TPU v7x, 32 devices: a whole 2x2x4 slice. The times are simulated.
32 devices in a mesh: grp: 2 (over core), rep: 16 (over z, y, x).
Axes of the slice: x: 2, y: 2, z: 4, core: 2. Of those that a mesh axis runs over, the one named last changes fastest.
Arguments:
- tokens: bfloat16 [16, 1024, 1152], P('rep', 'grp'), may hold values from -6 to 6
- cotangent: bfloat16 [16, 1024, 1152], P('rep', 'grp'), may hold values from -6 to 6
- segment_ids: int32 [16, 1024], P('rep'), may hold values from 0 to 3, never falling along the last dimension, each value on 1 to 800 neighbouring positions
- adapter_ids: int32 [16], P('rep'), may hold values from 0 to 7
- norm_gains: bfloat16 [2, 1152], P(None, 'grp'), may hold values from 0.5 to 1.5
- frozen_qkv: bfloat16 [1152, 1920], P('grp'), may hold values from -0.1875 to 0.1875
- frozen_out: bfloat16 [1152, 1152], P('grp'), may hold values from -1.5 to 1.5
- frozen_gate_up: bfloat16 [1152, 6144], P('grp'), may hold values from -0.1875 to 0.1875
- frozen_down: bfloat16 [3072, 1152], P('grp'), may hold values from -0.109375 to 0.109375
- lower_mats: bfloat16 [6, 8, 1152, 16], replicated, may hold values from -0.1875 to 0.1875
- lower_down: bfloat16 [8, 3072, 16], replicated, may hold values from -0.109375 to 0.109375
- upper_width: bfloat16 [3, 8, 16, 1152], replicated, may hold values from -1 to 1
- upper_keys: bfloat16 [2, 8, 16, 384], replicated, may hold values from -1 to 1
- upper_hidden: bfloat16 [2, 8, 16, 3072], replicated, may hold values from -1 to 1
Outputs:
- layer_out: bfloat16 [16, 1024, 1152], P('rep', 'grp')
- input_grad: bfloat16 [16, 1024, 1152], P('rep', 'grp')
- lower_grad: float32 [6, 8, 1152, 16], P(None, 'grp', 'rep')
- lower_down_grad: float32 [8, 3072, 16], P('grp', 'rep')
- upper_width_grad: float32 [3, 8, 16, 1152], P(None, 'grp', None, 'rep')
- upper_keys_grad: float32 [2, 8, 16, 384], P(None, 'grp', None, 'rep')
- upper_hidden_grad: float32 [2, 8, 16, 3072], P(None, 'grp', None, 'rep')
Inputs may be any that keep to these rules, and one draw needn't show every extreme that they name: `segment_ids`: within each sequence the ids never fall, each document has 1 to 800 positions, and one has exactly 800.
All inputs are finite; a program needn't handle non-finite values.
Results may differ from a plain program's by a relative error of at most 0.018.
Values may be sent and summed in bfloat16 or wider, within the bound.
No kernel may reach another device: no remote copies, remote signals or barrier semaphores. Data moves between devices by JAX's collectives and lax.ppermute only.
A program may use at most 192 MiB of HBM per device.

v0:
```python
import functools

import jax
import jax.numpy as jnp
import numpy as np
from jax import lax
from jax.experimental import pallas as pl
from jax.experimental.pallas import tpu as pltpu
from jax.sharding import PartitionSpec as P

D = 1152
H = 18
KVH = 6
HD = 64
FF = 3072
R = 16
NAD = 8
KV = 384

HALF = D // 2
HEADS = H // 2
GROUP = H // KVH
QW = 640
KW = 256
SPAN = QW + 2 * KW
AUG = D + 128
TILE = 512
BLOCK = 256
DOCS = 4
KEYS = HEADS // GROUP
VMEM_BYTES = 61900 * 1024

epsilon = 1e-05
theta_base = 10000.0
masked_value = -1e30
f32 = jnp.float32
bf16 = jnp.bfloat16
SWAP = [(0, 1), (1, 0)]

HBM = pl.BlockSpec(memory_space=pltpu.MemorySpace.HBM)
ANY = pl.BlockSpec(memory_space=pl.ANY)
VMEM = pl.BlockSpec(memory_space=pltpu.VMEM)
SMEM = pl.BlockSpec(memory_space=pltpu.SMEM)


def nn(left, right):
    return jnp.dot(left, right, preferred_element_type=f32)


def nt(left, right):
    return lax.dot_general(left, right, (((1,), (1,)), ((), ())), preferred_element_type=f32)


def tn(left, right):
    return lax.dot_general(left, right, (((0,), (0,)), ((), ())), preferred_element_type=f32)


def lanes(shape):
    return lax.broadcasted_iota(jnp.int32, shape, len(shape) - 1)


def gain_row(g, own, other, row):
    mine = own[row : row + 1, :].astype(f32)
    theirs = other[row : row + 1, :].astype(f32)
    return jnp.where(
        g == 0,
        jnp.concatenate([mine, theirs], axis=1),
        jnp.concatenate([theirs, mine], axis=1),
    )


def copied(source, target, sem):
    return pltpu.make_async_copy(source, target, sem)


def doc_starts(segments):
    return [
        jnp.sum(jnp.where(segments < doc, 1.0, 0.0), axis=-1, keepdims=True)
        for doc in range(1, DOCS)
    ]


def start_at(place, starts):
    found = jnp.zeros_like(place)
    for start in starts:
        found = jnp.where(place >= start, start, found)
    return found


def fill_angles(starts, cosine, sine):
    def both(angle):
        return jnp.cos(angle), jnp.sin(angle)

    powers = np.float32(theta_base) ** (-np.arange(HD // 2, dtype=np.float32) * 2.0 / HD)
    row = lax.broadcasted_iota(jnp.int32, (HD // 2, 128), 0)
    freqs = jnp.zeros(row.shape, f32)
    for index, power in enumerate(powers):
        freqs = jnp.where(row == index, np.float32(power), freqs)

    fine_cos, fine_sin = both(lanes(freqs.shape).astype(f32) * freqs)
    docs = [both(start * freqs) for start in starts]
    for at in range(0, cosine.shape[1], 128):
        wide_cos, wide_sin = both(float(at) * freqs)
        cos_p = wide_cos * fine_cos - wide_sin * fine_sin
        sin_p = wide_sin * fine_cos + wide_cos * fine_sin
        place = (lanes(freqs.shape) + at).astype(f32)
        cos_d, sin_d = jnp.ones_like(cos_p), jnp.zeros_like(cos_p)
        for start, (cos_s, sin_s) in zip(starts, docs):
            inside = place >= start
            cos_d = jnp.where(inside, cos_s, cos_d)
            sin_d = jnp.where(inside, sin_s, sin_d)
        cosine[:, at : at + 128] = cos_p * cos_d + sin_p * sin_d
        sine[:, at : at + 128] = sin_p * cos_d - cos_p * sin_d


def turned(block, cosine, sine):
    first, second = block[: HD // 2], block[HD // 2 :]
    return jnp.concatenate(
        [first * cosine - second * sine, second * cosine + first * sine], axis=0
    )


def head_rows(slot):
    return pl.ds(pl.multiple_of(slot * HD, HD), HD)


def fill_mask(bias, starts, low, high):
    place = lanes((1, BLOCK)).astype(f32) + low
    begin = start_at(place, starts)
    for first in range(0, high, BLOCK):
        key_place = lax.broadcasted_iota(jnp.int32, (BLOCK, BLOCK), 0).astype(f32) + first
        allowed = key_place >= begin
        if first == low:
            allowed = allowed & (key_place <= place)
        bias[first : first + BLOCK, :] = jnp.where(allowed, 0.0, masked_value)


def qkv_loads(g, chosen, own, oth, upper_width, upper_keys, weight, sems):
    w_here = pl.ds(pl.multiple_of(g * HALF, 64), HALF)
    w_there = pl.ds(pl.multiple_of((1 - g) * HALF, 64), HALF)
    windows = (
        (pl.multiple_of(g * 512, 128), QW, 0),
        (pl.multiple_of(D + g * 128, 128), KW, QW),
        (pl.multiple_of(D + KV + g * 128, 128), KW, QW + KW),
    )
    loads = []
    for index, (at, width, to) in enumerate(windows):
        for part, (source, rows) in enumerate(((own, w_here), (oth, w_there))):
            loads.append(
                copied(
                    source.at[:, pl.ds(at, width)],
                    weight.at[rows, pl.ds(to, width)],
                    sems.at[2 * index + part],
                )
            )
    if upper_width is None:
        return loads
    loads.append(
        copied(
            upper_width.at[0, chosen, :, pl.ds(pl.multiple_of(g * 512, 128), QW)],
            weight.at[pl.ds(D, R), pl.ds(0, QW)],
            sems.at[6],
        )
    )
    for index in range(2):
        loads.append(
            copied(
                upper_keys.at[index, chosen, :, pl.ds(pl.multiple_of(g * 128, 128), KW)],
                weight.at[pl.ds(D + (index + 1) * R, R), pl.ds(QW + index * KW, KW)],
                sems.at[7 + index],
            )
        )
    return loads


def attend_kernel(
    adapter,
    tok_own,
    tok_oth,
    qkv_own,
    qkv_oth,
    lower_t,
    upper_width,
    upper_keys,
    gains_own,
    gains_oth,
    segments,
    o_own,
    o_send,
    q_out,
    k_out,
    v_out,
    o_out,
    n_out,
    zt_out,
    lse_out,
    cos_out,
    sin_out,
    tok,
    normed,
    weight,
    maps,
    query,
    key_t,
    value_t,
    key_rows,
    value_aug,
    mixed_t,
    mixed,
    scores,
    chances,
    bias,
    cosine,
    sine,
    inner_t,
    lse,
    sems,
    w_sems,
    out_sems,
):
    g = lax.axis_index("grp")
    chosen = adapter[0]
    rows = tok_own.shape[0]
    here = pl.ds(pl.multiple_of(g * rows, 128), rows)
    there = pl.ds(pl.multiple_of((1 - g) * rows, 128), rows)
    maps[...] = jnp.zeros_like(maps)
    weight[D:, :] = jnp.zeros((128, SPAN), bf16)
    loads = [
        copied(tok_own, tok.at[here], sems.at[0]),
        copied(tok_oth, tok.at[there], sems.at[1]),
    ] + [
        copied(lower_t.at[index, chosen], maps.at[pl.ds(index * R, R)], sems.at[2 + index])
        for index in range(3)
    ]
    w_loads = qkv_loads(g, chosen, qkv_own, qkv_oth, upper_width, upper_keys, weight, w_sems)
    for load in loads:
        load.start()
    starts = doc_starts(segments[...])
    fill_angles(starts, cosine, sine)
    gain = gain_row(g, gains_own, gains_oth, 0)
    for load in loads:
        load.wait()
    for load in w_loads:
        load.start()

    def norm_part(part, carry):
        span = pl.ds(pl.multiple_of(part * rows, 128), rows)
        wide = tok[span, :].astype(f32)
        scale = lax.rsqrt(jnp.mean(wide * wide, axis=-1, keepdims=True) + epsilon)
        normed[span, :D] = (wide * scale * gain).astype(bf16)
        inner = nt(normed[span, :D], maps[...])
        normed[span, D:] = inner.astype(bf16)
        inner_t[:, span] = inner.T[: 3 * R, :].astype(bf16)
        return carry

    lax.fori_loop(0, 2, norm_part, 0)
    for load in w_loads:
        load.wait()

    def project(part, carry):
        span = pl.ds(pl.multiple_of(part * rows, 128), rows)
        cos_cols = cosine[:, span]
        sin_cols = sine[:, span]
        for target, base, count, turn, scale in (
            (query, 0, QW, True, HD**-0.5),
            (key_t, QW, KW, True, 1.0),
            (value_t, QW + KW, KW, False, 1.0),
        ):
            for at in range(0, count, 256):
                width = min(256, count - at)
                made = nn(normed[span, :], weight[:, base + at : base + at + width]).T
                for to in range(0, width, HD):
                    block = made[to : to + HD]
                    if turn:
                        block = turned(block, cos_cols, sin_cols) * scale
                    target[at + to : at + to + HD, span] = block.astype(bf16)
        return carry

    lax.fori_loop(0, 2, project, 0)
    stores = [
        copied(query, q_out, out_sems.at[0]),
        copied(key_t, k_out, out_sems.at[1]),
        copied(value_t, v_out, out_sems.at[2]),
        copied(normed.at[:, pl.ds(0, D)], n_out, out_sems.at[3]),
        copied(cosine, cos_out, out_sems.at[4]),
        copied(sine, sin_out, out_sems.at[5]),
        copied(inner_t, zt_out, out_sems.at[6]),
    ]
    for store in stores:
        store.start()
    for j in range(KEYS):
        key_rows[j] = key_t[head_rows(j + g), :].T
        value_aug[j, :HD, :] = value_t[head_rows(j + g), :]
        value_aug[j, HD:, :] = jnp.ones((R, 2 * rows), bf16)
    mixed_t[:HD, :] = jnp.zeros((HD, 2 * rows), bf16)
    mixed_t[(HEADS + 1) * HD :, :] = jnp.zeros((HD, 2 * rows), bf16)

    for block in range(2 * rows // BLOCK):
        low, high = block * BLOCK, (block + 1) * BLOCK
        fill_mask(bias, starts, low, high)

        def score(h, side, low=low, high=high):
            top = None
            for first in range(0, high, BLOCK):
                span = slice(first, first + BLOCK)
                made = (
                    nn(key_rows[h // GROUP, span, :], query[head_rows(h + g), low:high])
                    + bias[span, :]
                )
                scores[side, span, :] = made
                best = jnp.max(made.reshape(BLOCK // 8, 8, BLOCK), axis=0)
                top = best if top is None else jnp.maximum(top, best)
            return jnp.max(top, axis=0, keepdims=True)

        def blend(h, side, top, low=low, high=high):
            for first in range(0, high, BLOCK):
                span = slice(first, first + BLOCK)
                chances[side, span, :] = jnp.exp(scores[side, span, :] - top).astype(bf16)
            made = nn(value_aug[h // GROUP, :, :high], chances[side, :high, :])
            total = made[HD : HD + 1]
            mixed_t[head_rows(h + 1), low:high] = (made[:HD] * (1.0 / total)).astype(bf16)
            lse[pl.ds(h, 1), low:high] = top + jnp.log(total)

        def group(j, top, score=score, blend=blend):
            for member in range(GROUP):
                h = j * GROUP + member
                later = score(jnp.minimum(h + 1, HEADS - 1), (member + 1) % GROUP)
                blend(h, member, top)
                top = later
            return top

        lax.fori_loop(0, KEYS, group, score(0, 0))
        for pair in range(QW // 128):
            side = pl.ds(pl.multiple_of((2 * pair + 1 - g) * HD, HD), 128)
            mixed[low:high, pair * 128 : pair * 128 + 128] = mixed_t[side, low:high].T
    stores += [
        copied(mixed.at[here], o_own, out_sems.at[7]),
        copied(mixed.at[there], o_send, out_sems.at[8]),
        copied(mixed_t, o_out, out_sems.at[9]),
        copied(lse, lse_out, out_sems.at[10]),
    ]
    for store in stores[-4:]:
        store.start()
    for store in stores:
        store.wait()


def attend(adapter, tok_own, *rest):
    rows = tok_own.shape[0]
    length = 2 * rows
    shape = jax.ShapeDtypeStruct
    return pl.pallas_call(
        attend_kernel,
        out_shape=[
            shape((rows, QW), bf16),
            shape((rows, QW), bf16),
            shape((QW, length), bf16),
            shape((KW, length), bf16),
            shape((KW, length), bf16),
            shape(((HEADS + 2) * HD, length), bf16),
            shape((length, D), bf16),
            shape((3 * R, length), bf16),
            shape((R, length), f32),
            shape((HD // 2, length), f32),
            shape((HD // 2, length), f32),
        ],
        in_specs=[SMEM, HBM, ANY, HBM, ANY] + [HBM] * 3 + [VMEM] * 3,
        out_specs=[HBM] * 11,
        scratch_shapes=[
            pltpu.VMEM((length, D), bf16),
            pltpu.VMEM((length, AUG), bf16),
            pltpu.VMEM((AUG, SPAN), bf16),
            pltpu.VMEM((128, D), bf16),
            pltpu.VMEM((QW, length), bf16),
            pltpu.VMEM((KW, length), bf16),
            pltpu.VMEM((KW, length), bf16),
            pltpu.VMEM((KEYS, length, HD), bf16),
            pltpu.VMEM((KEYS, HD + R, length), bf16),
            pltpu.VMEM(((HEADS + 2) * HD, length), bf16),
            pltpu.VMEM((length, QW), bf16),
            pltpu.VMEM((GROUP, length, BLOCK), f32),
            pltpu.VMEM((GROUP, length, BLOCK), bf16),
            pltpu.VMEM((length, BLOCK), f32),
            pltpu.VMEM((HD // 2, length), f32),
            pltpu.VMEM((HD // 2, length), f32),
            pltpu.VMEM((3 * R, length), bf16),
            pltpu.VMEM((R, length), f32),
            pltpu.SemaphoreType.DMA((5,)),
            pltpu.SemaphoreType.DMA((9,)),
            pltpu.SemaphoreType.DMA((11,)),
        ],
        compiler_params=pltpu.CompilerParams(vmem_limit_bytes=VMEM_BYTES),
        cost_estimate=pl.CostEstimate(
            flops=16 * 10**9, bytes_accessed=16 << 20, transcendentals=6 * 10**6
        ),
        name="attend",
    )(adapter, tok_own, *rest)


def normed_back(rows, gain_row, grad):
    scale = lax.rsqrt(jnp.mean(rows * rows, axis=-1, keepdims=True) + epsilon)
    scaled = grad * gain_row
    inside = jnp.mean(rows * scaled, axis=-1, keepdims=True)
    return scale * (scaled - rows * (scale * scale * inside))


def rounded_up(count, unit):
    return -(-count // unit) * unit


def feed_lanes(reps):
    return rounded_up((5 * D + 3 * FF) // reps, 256)


def qkv_lanes(reps):
    return rounded_up((4 * D + 2 * KV) // reps + 1, 128)


def packed(grads, reps, target):
    for rep in range(reps):
        at = 0
        for grad in grads:
            piece = grad.shape[-1] // reps
            share = grad[:, rep * piece : (rep + 1) * piece]
            target[rep * R : (rep + 1) * R, at : at + piece] = share.astype(target.dtype)
            at += piece


def feed_kernel(
    reps,
    adapter,
    o_own_in,
    o_oth_in,
    tok_in,
    cot_in,
    wo_own,
    wo_oth,
    wgu_own,
    wgu_oth,
    wd_own,
    wd_oth,
    a_down,
    lower_t,
    upper_width,
    upper_hidden,
    gains_own,
    gains_oth,
    layer_out,
    grad_middle,
    do_own_out,
    do_oth_out,
    pack_own_out,
    pack_send_out,
    o_own,
    o_oth,
    tok,
    cot,
    do_own,
    do_oth,
    wout,
    wg,
    wu,
    wd,
    at_out,
    at_gu,
    b_out,
    b_down,
    middle,
    normed,
    cot_aug,
    total,
    back,
    result,
    z_gu_t,
    dz_down_t,
    ga_out,
    gb_gate,
    gb_up,
    ga_down,
    pack,
    sems,
    o_sems,
    out_sems,
):
    g = lax.axis_index("grp")
    chosen = adapter[0]
    gain = gain_row(g, gains_own, gains_oth, 1)
    steps = FF // TILE
    each = steps // 2
    w_here = pl.ds(pl.multiple_of(g * HALF, 64), HALF)
    w_there = pl.ds(pl.multiple_of((1 - g) * HALF, 64), HALF)

    def column(step):
        owner = jnp.where(step < each, g, 1 - g)
        return owner * (FF // 2) + (step % each) * TILE

    def copies(step, slot):
        at = pl.multiple_of(column(step), TILE)
        gate_at = pl.ds(at, TILE)
        up_at = pl.ds(pl.multiple_of(FF + at, TILE), TILE)
        sem = lambda k: sems.at[slot, k]
        return [
            copied(wgu_own.at[:, gate_at], wg.at[slot, w_here], sem(0)),
            copied(wgu_oth.at[:, gate_at], wg.at[slot, w_there], sem(1)),
            copied(wgu_own.at[:, up_at], wu.at[slot, w_here], sem(2)),
            copied(wgu_oth.at[:, up_at], wu.at[slot, w_there], sem(3)),
            copied(upper_hidden.at[0, chosen, :, gate_at], wg.at[slot, pl.ds(D, R)], sem(4)),
            copied(upper_hidden.at[1, chosen, :, gate_at], wu.at[slot, pl.ds(D + R, R)], sem(5)),
            copied(a_down.at[gate_at], wd.at[slot, :, pl.ds(D, 128)], sem(6)),
        ]

    def down_copy(source, step, slot):
        local = pl.ds(pl.multiple_of((step % each) * TILE, TILE), TILE)
        return copied(source.at[local], wd.at[slot, :, pl.ds(0, D)], sems.at[slot, 7])

    def start(step, slot):
        for copy in copies(step, slot):
            copy.start()

        @pl.when(step < each)
        def _():
            down_copy(wd_own, step, slot).start()

        @pl.when(step >= each)
        def _():
            down_copy(wd_oth, step, slot).start()

    def wait(step, slot):
        for copy in copies(step, slot):
            copy.wait()
        down_copy(wd_own, step, slot).wait()

    for slot in range(2):
        wg[slot, D:, :] = jnp.zeros((128, TILE), bf16)
        wu[slot, D:, :] = jnp.zeros((128, TILE), bf16)
        at_out[slot] = jnp.zeros((128, QW), bf16)
        wout[slot, :HD, :D] = jnp.zeros((HD, D), bf16)
        wout[slot, HALF:, :D] = jnp.zeros((HD, D), bf16)
    for ref in (at_gu, b_out, b_down):
        ref[...] = jnp.zeros_like(ref)
    own_at = pl.multiple_of(g * 512, 128)
    oth_at = pl.multiple_of((1 - g) * 512, 128)
    loads = [
        copied(
            wo_own, wout.at[0, pl.ds(pl.multiple_of(g * HD, HD), HALF), pl.ds(0, D)], o_sems.at[0]
        ),
        copied(
            wo_oth,
            wout.at[1, pl.ds(pl.multiple_of((1 - g) * HD, HD), HALF), pl.ds(0, D)],
            o_sems.at[1],
        ),
        copied(lower_t.at[3, chosen, :, pl.ds(own_at, QW)], at_out.at[0, pl.ds(0, R)], o_sems.at[2]),
        copied(lower_t.at[3, chosen, :, pl.ds(oth_at, QW)], at_out.at[1, pl.ds(0, R)], o_sems.at[3]),
        copied(lower_t.at[4, chosen], at_gu.at[pl.ds(0, R)], o_sems.at[4]),
        copied(lower_t.at[5, chosen], at_gu.at[pl.ds(R, R)], o_sems.at[5]),
        copied(upper_width.at[1, chosen], b_out.at[pl.ds(0, R)], o_sems.at[6]),
        copied(upper_width.at[2, chosen], b_down.at[pl.ds(0, R)], o_sems.at[7]),
        copied(o_own_in, o_own, o_sems.at[8]),
        copied(o_oth_in, o_oth, o_sems.at[9]),
        copied(tok_in, tok, o_sems.at[10]),
        copied(cot_in, cot, o_sems.at[11]),
    ]
    first, second, third = loads[11:] + loads[2:4] + loads[7:8], loads[:2] + loads[8:10], loads[4:7] + loads[10:11]
    for load in first + second + third:
        load.start()
    total[...] = jnp.zeros_like(total)
    back[...] = jnp.zeros_like(back)
    for load in first:
        load.wait()
    cot_aug[:, :D] = cot[...]
    dz_down = nt(cot[...], b_down[...])
    cot_aug[:, D:] = dz_down.astype(bf16)
    dz_down_t[...] = dz_down.T[:R, :].astype(bf16)
    for slot in range(2):
        wout[slot, :, D:] = at_out[slot].T
    for load in second + third:
        load.wait()
    start(0, 0)
    made = nn(o_own[...], wout[0]) + nn(o_oth[...], wout[1])
    inner_out = made[:, D:].astype(bf16)
    middle[...] = tok[...].astype(f32) + made[:, :D] + nn(inner_out, b_out[...])
    scale = lax.rsqrt(jnp.mean(middle[...] * middle[...], axis=-1, keepdims=True) + epsilon)
    normed[:, :D] = (middle[...] * scale * gain).astype(bf16)
    inner_gu = nt(normed[:, :D], at_gu[...])
    normed[:, D:] = inner_gu.astype(bf16)
    z_gu_t[...] = inner_gu.T[: 2 * R, :].astype(bf16)

    def step_body(step, carry):
        slot = step % 2

        @pl.when(step + 1 < steps)
        def _():
            start(step + 1, 1 - slot)

        wait(step, slot)
        gate_at = pl.ds(pl.multiple_of(column(step), TILE), TILE)
        gate = nn(normed[...], wg[slot])
        up = nn(normed[...], wu[slot])
        grad_active = nt(cot_aug[...], wd[slot])
        sigmoid = 1.0 / (1.0 + jnp.exp(-gate))
        silu = gate * sigmoid
        active = (silu * up).astype(bf16)
        grad_gate = (grad_active * up * (sigmoid * (1.0 + gate * (1.0 - sigmoid)))).astype(bf16)
        grad_up = (grad_active * silu).astype(bf16)
        total[...] += nn(active, wd[slot])
        back[...] += nt(grad_gate, wg[slot]) + nt(grad_up, wu[slot])
        gb_gate[:, gate_at] = nn(z_gu_t[...], grad_gate)[:R]
        gb_up[:, gate_at] = nn(z_gu_t[...], grad_up)[R:]
        ga_down[:, gate_at] = nn(dz_down_t[...], active)
        return carry

    lax.fori_loop(0, steps, step_body, 0)

    inner_down = total[:, D:].astype(bf16)
    result[...] = (middle[...] + total[:, :D] + nn(inner_down, b_down[...])).astype(bf16)
    stores = [copied(result, layer_out, out_sems.at[0])]
    stores[0].start()
    gb_down = nn(total[:, D:].T[:R, :].astype(bf16), cot[...])
    dz_gu = back[:, D:].astype(bf16)
    grad_normed = back[:, :D] + nn(dz_gu, at_gu[...])
    grad = cot[...].astype(f32) + normed_back(middle[...], gain, grad_normed)
    total[:, :D] = grad
    stores.append(copied(total.at[:, pl.ds(0, D)], grad_middle, out_sems.at[1]))
    stores[1].start()
    branch = normed
    ga_gu = nn(back[:, D:].T[: 2 * R, :].astype(bf16), normed[:, :D])
    branch[:, :D] = grad.astype(bf16)
    dz_out = nt(branch[:, :D], b_out[...])
    branch[:, D:] = dz_out.astype(bf16)
    dz_out_t = dz_out.T[:R, :].astype(bf16)
    do_oth[...] = nt(wout[1], branch[...]).astype(bf16)
    stores.append(copied(do_oth, do_oth_out, out_sems.at[2]))
    stores[-1].start()
    do_own[...] = nt(wout[0], branch[...]).astype(bf16)
    stores.append(copied(do_own, do_own_out, out_sems.at[3]))
    stores[-1].start()
    gb_out = nn(inner_out.astype(f32).T[:R, :].astype(bf16), branch[:, :D])
    ga_out[...] = jnp.zeros_like(ga_out)
    ga_out[:, pl.ds(own_at, QW)] += nn(dz_out_t, o_own[...])
    ga_out[:, pl.ds(oth_at, QW)] += nn(dz_out_t, o_oth[...])
    pack[...] = jnp.zeros_like(pack)
    packed(
        [ga_out[...], ga_gu[:R], ga_gu[R:], gb_out, gb_down, ga_down[...], gb_gate[...], gb_up[...]],
        reps,
        pack,
    )
    half = pack.shape[1] // 2
    for index, (side, target) in enumerate(((g, pack_own_out), (1 - g, pack_send_out))):
        source = pack.at[:, pl.ds(pl.multiple_of(side * half, 128), half)]
        stores.append(copied(source, target, out_sems.at[4 + index]))
        stores[-1].start()
    for store in stores:
        store.wait()


def feed(reps, *args):
    rows = args[3].shape[0]
    half = feed_lanes(reps) // 2
    shape = jax.ShapeDtypeStruct
    return pl.pallas_call(
        functools.partial(feed_kernel, reps),
        out_shape=[
            shape((rows, D), bf16),
            shape((rows, D), f32),
            shape((QW, rows), bf16),
            shape((QW, rows), bf16),
            shape((reps * R, half), bf16),
            shape((reps * R, half), bf16),
        ],
        in_specs=[SMEM, HBM, ANY] + [HBM] * 12 + [VMEM] * 2,
        out_specs=[HBM] * 6,
        scratch_shapes=[
            pltpu.VMEM((rows, QW), bf16),
            pltpu.VMEM((rows, QW), bf16),
            pltpu.VMEM((rows, D), bf16),
            pltpu.VMEM((rows, D), bf16),
            pltpu.VMEM((QW, rows), bf16),
            pltpu.VMEM((QW, rows), bf16),
            pltpu.VMEM((2, QW, AUG), bf16),
            pltpu.VMEM((2, AUG, TILE), bf16),
            pltpu.VMEM((2, AUG, TILE), bf16),
            pltpu.VMEM((2, TILE, AUG), bf16),
            pltpu.VMEM((2, 128, QW), bf16),
            pltpu.VMEM((128, D), bf16),
            pltpu.VMEM((128, D), bf16),
            pltpu.VMEM((128, D), bf16),
            pltpu.VMEM((rows, D), f32),
            pltpu.VMEM((rows, AUG), bf16),
            pltpu.VMEM((rows, AUG), bf16),
            pltpu.VMEM((rows, AUG), f32),
            pltpu.VMEM((rows, AUG), f32),
            pltpu.VMEM((rows, D), bf16),
            pltpu.VMEM((2 * R, rows), bf16),
            pltpu.VMEM((R, rows), bf16),
            pltpu.VMEM((R, D), f32),
            pltpu.VMEM((R, FF), f32),
            pltpu.VMEM((R, FF), f32),
            pltpu.VMEM((R, FF), f32),
            pltpu.VMEM((reps * R, 2 * half), bf16),
            pltpu.SemaphoreType.DMA((2, 8)),
            pltpu.SemaphoreType.DMA((12,)),
            pltpu.SemaphoreType.DMA((6,)),
        ],
        compiler_params=pltpu.CompilerParams(vmem_limit_bytes=56 << 20),
        cost_estimate=pl.CostEstimate(
            flops=30 * 10**9, bytes_accessed=36 << 20, transcendentals=2 * 10**6
        ),
        name="feed",
    )(*args)


def attend_back_kernel(
    reps,
    adapter,
    do_own,
    do_oth,
    o_in,
    normed,
    qkv_own,
    qkv_oth,
    lower_t,
    upper_width,
    upper_keys,
    query_in,
    k_in,
    v_in,
    zt_in,
    lse_in,
    cos_in,
    sin_in,
    segments,
    pack_own_in,
    pack_oth_in,
    dy_out,
    dz_out,
    part_out,
    exchange_out,
    query,
    key_t,
    value_t,
    zt,
    lse,
    cosine,
    sine,
    pack_own,
    pack_oth,
    inner_low,
    exchange,
    outgoing,
    maps,
    grad_o,
    mixed_t,
    n_rows,
    weight,
    key_rows,
    value_rows,
    delta,
    dq,
    dk,
    dv,
    dy_t,
    dy,
    chances,
    grad_scores,
    bias,
    gb_q,
    gb_kv,
    pack,
    sems,
    b_sems,
    out_sem,
):
    g = lax.axis_index("grp")
    chosen = adapter[0]
    length = query.shape[1]
    rows = length // 2
    here = pl.ds(pl.multiple_of(g * rows, 128), rows)
    there = pl.ds(pl.multiple_of((1 - g) * rows, 128), rows)
    weight[D:, :] = jnp.zeros((128, SPAN), bf16)
    maps[...] = jnp.zeros_like(maps)
    early = [
        copied(k_in, key_t, sems.at[0]),
        copied(v_in, value_t, sems.at[1]),
    ]
    loads = [
        copied(do_own, grad_o.at[:, here], sems.at[2]),
        copied(do_oth, grad_o.at[:, there], sems.at[3]),
        copied(o_in, mixed_t, sems.at[4]),
        copied(query_in, query, sems.at[5]),
        copied(lse_in, lse, sems.at[6]),
    ]
    late = [
        copied(cos_in, cosine, sems.at[7]),
        copied(sin_in, sine, sems.at[8]),
        copied(normed, n_rows, sems.at[9]),
        copied(zt_in, zt, sems.at[10]),
        copied(pack_own_in, pack_own, sems.at[11]),
        copied(pack_oth_in, pack_oth, sems.at[12]),
    ] + [
        copied(lower_t.at[index, chosen], maps.at[pl.ds(index * R, R)], sems.at[13 + index])
        for index in range(3)
    ] + qkv_loads(g, chosen, qkv_own, qkv_oth, upper_width, upper_keys, weight, b_sems)
    for load in early + loads:
        load.start()
    dk[...] = jnp.zeros_like(dk)
    dv[...] = jnp.zeros_like(dv)
    dy_t[...] = jnp.zeros_like(dy_t)
    starts = doc_starts(segments[...])
    for load in early:
        load.wait()
    for j in range(KEYS):
        key_rows[j] = key_t[head_rows(j + g), :].T
        value_rows[j] = value_t[head_rows(j + g), :].T
    for load in loads:
        load.wait()
    for load in late:
        load.start()
    for h in range(HEADS):
        product = grad_o[head_rows(h + g), :].astype(f32) * mixed_t[
            (h + 1) * HD : (h + 2) * HD, :
        ].astype(f32)
        delta[h : h + 1, :] = jnp.sum(product, axis=0, keepdims=True)

    for block in range(length // BLOCK):
        low, high = block * BLOCK, (block + 1) * BLOCK
        fill_mask(bias, starts, low, high)

        def score(h, side, low=low, high=high):
            logs = lse[pl.ds(h, 1), low:high]
            deltas = delta[pl.ds(h, 1), low:high]
            for first in range(0, high, BLOCK):
                span = slice(first, first + BLOCK)
                made = nn(key_rows[h // GROUP, span, :], query[head_rows(h + g), low:high])
                grad = nn(value_rows[h // GROUP, span, :], grad_o[head_rows(h + g), low:high])
                chance = jnp.exp(made + bias[span, :] - logs)
                chances[side, span, :] = chance.astype(bf16)
                grad_scores[side, span, :] = (chance * (grad - deltas)).astype(bf16)

        def spread(h, side, low=low, high=high):
            dq[h, :, low:high] = nn(
                key_t[head_rows(h // GROUP + g), :high], grad_scores[side, :high, :]
            )
            return (
                nt(grad_o[head_rows(h + g), low:high], chances[side, :high, :]),
                nt(query[head_rows(h + g), low:high], grad_scores[side, :high, :]),
            )

        def group(j, carry, high=high, score=score, spread=spread):
            found = []
            for member in range(GROUP):
                h = j * GROUP + member
                score(jnp.minimum(h + 1, HEADS - 1), (member + 1) % GROUP)
                found.append(spread(h, member))
            dv[j, :, :high] += found[0][0] + found[1][0] + found[2][0]
            dk[j, :, :high] += found[0][1] + found[1][1] + found[2][1]
            return carry

        score(0, 0)
        lax.fori_loop(0, KEYS, group, 0)

    for load in late:
        load.wait()
    back_sine = -sine[...]
    for h in range(HEADS):
        dy_t[(h + 1) * HD : (h + 2) * HD, :] = (
            turned(dq[h], cosine[...], back_sine) * HD**-0.5
        ).astype(bf16)
    key_base = (HEADS + 2) * HD
    value_base = key_base + (KEYS + 2) * HD
    for j in range(KEYS):
        at = key_base + (j + 1) * HD
        dy_t[at : at + HD, :] = turned(dk[j], cosine[...], back_sine).astype(bf16)
        at = value_base + (j + 1) * HD
        dy_t[at : at + HD, :] = dv[j].astype(bf16)
    for base, count, to in ((0, QW, 0), (key_base, KW, QW), (value_base, KW, QW + KW)):
        for at in range(0, count, 128):
            side = pl.ds(pl.multiple_of(base + at + (1 - g) * HD, HD), 128)
            dy[:, to + at : to + at + 128] = dy_t[side, :].T
    store = copied(dy.at[here], dy_out, out_sem.at[0])
    store.start()
    made = nt(dy[there, :], weight[...])
    theirs = made[:, D:]
    outgoing[...] = (made[:, :D] + nn(theirs.astype(bf16), maps[...])).astype(bf16)
    part_store = copied(outgoing, part_out, out_sem.at[3])
    part_store.start()
    mine = nt(dy[here, :], weight[D:, :])
    inner_low[...] = mine.astype(bf16)
    inner_store = copied(inner_low, dz_out, out_sem.at[1])
    inner_store.start()
    gb = nn(zt[...], dy[...])
    gb_q[...] = jnp.zeros_like(gb_q)
    gb_kv[...] = jnp.zeros_like(gb_kv)
    gb_q[:, pl.ds(pl.multiple_of(g * 512, 128), QW)] = gb[:R, :QW]
    for index in range(2):
        gb_kv[index, :, pl.ds(pl.multiple_of(g * 128, 128), KW)] = gb[
            (index + 1) * R : (index + 2) * R, QW + index * KW : QW + (index + 1) * KW
        ]
    ga = nn(theirs.T[: 3 * R, :].astype(bf16), n_rows[there, :]) + nn(
        mine.T[: 3 * R, :].astype(bf16), n_rows[here, :]
    )
    pack[...] = jnp.zeros_like(pack)
    packed(
        [ga[:R], ga[R : 2 * R], ga[2 * R :], gb_q[...], gb_kv[0], gb_kv[1]],
        reps,
        pack,
    )
    half = pack_own.shape[1]
    width = pack.shape[1]
    exchange[:, :half] = (pack_own[...].astype(f32) + pack_oth[...].astype(f32)).astype(bf16)
    exchange[:, half:] = jnp.where(
        lanes(pack.shape) == width - 1, chosen.astype(f32), pack[...].astype(f32)
    ).astype(bf16)
    last = copied(exchange, exchange_out, out_sem.at[2])
    last.start()
    for copy in (store, inner_store, part_store, last):
        copy.wait()


def attend_back(reps, *args):
    rows = args[1].shape[1]
    length = 2 * rows
    half = feed_lanes(reps) // 2
    width = qkv_lanes(reps)
    shape = jax.ShapeDtypeStruct
    return pl.pallas_call(
        functools.partial(attend_back_kernel, reps),
        out_shape=[
            shape((rows, SPAN), bf16),
            shape((rows, 128), bf16),
            shape((rows, D), bf16),
            shape((reps * R, half + width), bf16),
        ],
        in_specs=[SMEM, HBM, ANY] + [HBM] * 14 + [VMEM, HBM, ANY],
        out_specs=[HBM] * 4,
        scratch_shapes=[
            pltpu.VMEM((QW, length), bf16),
            pltpu.VMEM((KW, length), bf16),
            pltpu.VMEM((KW, length), bf16),
            pltpu.VMEM((3 * R, length), bf16),
            pltpu.VMEM((R, length), f32),
            pltpu.VMEM((HD // 2, length), f32),
            pltpu.VMEM((HD // 2, length), f32),
            pltpu.VMEM((reps * R, half), bf16),
            pltpu.VMEM((reps * R, half), bf16),
            pltpu.VMEM((rows, 128), bf16),
            pltpu.VMEM((reps * R, half + width), bf16),
            pltpu.VMEM((rows, D), bf16),
            pltpu.VMEM((128, D), bf16),
            pltpu.VMEM((QW, length), bf16),
            pltpu.VMEM(((HEADS + 2) * HD, length), bf16),
            pltpu.VMEM((length, D), bf16),
            pltpu.VMEM((AUG, SPAN), bf16),
            pltpu.VMEM((KEYS, length, HD), bf16),
            pltpu.VMEM((KEYS, length, HD), bf16),
            pltpu.VMEM((R, length), f32),
            pltpu.VMEM((HEADS, HD, length), f32),
            pltpu.VMEM((KEYS, HD, length), f32),
            pltpu.VMEM((KEYS, HD, length), f32),
            pltpu.VMEM(((HEADS + 2 * KEYS + 6) * HD, length), bf16),
            pltpu.VMEM((length, SPAN), bf16),
            pltpu.VMEM((GROUP, length, BLOCK), bf16),
            pltpu.VMEM((GROUP, length, BLOCK), bf16),
            pltpu.VMEM((length, BLOCK), f32),
            pltpu.VMEM((R, D), f32),
            pltpu.VMEM((2, R, KV), f32),
            pltpu.VMEM((reps * R, width), bf16),
            pltpu.SemaphoreType.DMA((16,)),
            pltpu.SemaphoreType.DMA((9,)),
            pltpu.SemaphoreType.DMA((4,)),
        ],
        compiler_params=pltpu.CompilerParams(vmem_limit_bytes=56 << 20),
        cost_estimate=pl.CostEstimate(
            flops=24 * 10**9, bytes_accessed=20 << 20, transcendentals=6 * 10**6
        ),
        name="attend_back",
    )(*args)


def finish_kernel(
    adapter,
    dy_in,
    dz_in,
    qkv_own,
    qkv_oth,
    lower_t,
    tok_in,
    gains_own,
    gains_oth,
    part_in,
    middle_in,
    out,
    dy,
    dz,
    tok,
    part,
    grad_middle,
    weight,
    maps,
    result,
    sems,
    w_sems,
    out_sem,
):
    g = lax.axis_index("grp")
    chosen = adapter[0]
    maps[...] = jnp.zeros_like(maps)
    loads = qkv_loads(g, chosen, qkv_own, qkv_oth, None, None, weight, w_sems)
    for index, (source, target) in enumerate(
        ((dy_in, dy), (dz_in, dz), (tok_in, tok), (middle_in, grad_middle), (part_in, part))
    ):
        loads.append(copied(source, target, sems.at[index]))
    for index in range(3):
        loads.append(
            copied(lower_t.at[index, chosen], maps.at[pl.ds(index * R, R)], sems.at[5 + index])
        )
    for load in loads:
        load.start()
    gain = gain_row(g, gains_own, gains_oth, 0)
    for load in loads:
        load.wait()

    def half(index, carry):
        count = tok.shape[0] // 2
        span = pl.ds(pl.multiple_of(index * count, 128), count)
        grad = nt(dy[span, :], weight[...]) + nn(dz[span, :], maps[...]) + part[span, :].astype(f32)
        result[span, :] = (
            grad_middle[span, :] + normed_back(tok[span, :].astype(f32), gain, grad)
        ).astype(bf16)
        return carry

    lax.fori_loop(0, 2, half, 0)
    store = copied(result, out, out_sem.at[0])
    store.start()
    store.wait()


def finish(*args):
    rows = args[1].shape[0]
    return pl.pallas_call(
        finish_kernel,
        out_shape=jax.ShapeDtypeStruct((rows, D), bf16),
        in_specs=[SMEM] + [HBM] * 6 + [VMEM] * 2 + [ANY, HBM],
        out_specs=HBM,
        scratch_shapes=[
            pltpu.VMEM((rows, SPAN), bf16),
            pltpu.VMEM((rows, 128), bf16),
            pltpu.VMEM((rows, D), bf16),
            pltpu.VMEM((rows, D), bf16),
            pltpu.VMEM((rows, D), f32),
            pltpu.VMEM((D, SPAN), bf16),
            pltpu.VMEM((128, D), bf16),
            pltpu.VMEM((rows, D), bf16),
            pltpu.SemaphoreType.DMA((8,)),
            pltpu.SemaphoreType.DMA((6,)),
            pltpu.SemaphoreType.DMA((1,)),
        ],
        compiler_params=pltpu.CompilerParams(vmem_limit_bytes=VMEM_BYTES),
        cost_estimate=pl.CostEstimate(
            flops=4 * 10**9, bytes_accessed=10 << 20, transcendentals=0
        ),
        name="finish",
    )(*args)


def collect_kernel(source, keep, send, received, sem):
    load = copied(source, received, sem.at[0])
    load.start()
    load.wait()
    g = lax.axis_index("grp")
    count, width = received.shape
    quota = NAD // 2
    label = received[:, width - 1 :].astype(f32)
    lane = lanes((count, NAD * R))
    row = lax.broadcasted_iota(jnp.int32, (count, NAD * R), 0)
    picks = ((lane // R).astype(f32) == label) & (lane % R == row % R)
    sums = tn(picks.astype(f32).astype(bf16), received[...])
    first = g == 0
    for adapter in range(quota):
        low = sums[adapter * R : (adapter + 1) * R]
        high = sums[(quota + adapter) * R : (quota + adapter + 1) * R]
        keep[adapter] = jnp.where(first, low, high)
        send[adapter] = jnp.where(first, high, low)


def collect(received):
    shape = jax.ShapeDtypeStruct((NAD // 2, R, received.shape[1]), f32)
    return pl.pallas_call(
        collect_kernel,
        out_shape=[shape, shape],
        in_specs=[ANY],
        out_specs=[VMEM] * 2,
        scratch_shapes=[
            pltpu.VMEM(received.shape, bf16),
            pltpu.SemaphoreType.DMA((1,)),
        ],
        compiler_params=pltpu.CompilerParams(vmem_limit_bytes=8 << 20),
        cost_estimate=pl.CostEstimate(flops=10**8, bytes_accessed=2 << 20, transcendentals=0),
        name="collect",
    )(received)


def deliver_kernel(reps, keep, other, lower, down, width, keys, hidden, feeds, qkvs):
    g = lax.axis_index("grp")
    half = feeds.shape[-1] // 2
    feeds[:, :, pl.ds(pl.multiple_of(g * half, 128), half)] = keep[:, :, :half]
    feeds[:, :, pl.ds(pl.multiple_of((1 - g) * half, 128), half)] = other[:, :, :half]
    qkvs[...] = keep[:, :, half:] + other[:, :, half:]
    piece, tall, short = D // reps, FF // reps, KV // reps
    for index in range(3):
        lower[index] = qkvs[:, :, index * piece : (index + 1) * piece]
        lower[3 + index] = feeds[:, :, index * piece : (index + 1) * piece]
    width[0] = qkvs[:, :, 3 * piece : 4 * piece]
    width[1] = feeds[:, :, 3 * piece : 4 * piece]
    width[2] = feeds[:, :, 4 * piece : 5 * piece]
    for index in range(2):
        at = 4 * piece + index * short
        keys[index] = qkvs[:, :, at : at + short]
        at = 5 * piece + (1 + index) * tall
        hidden[index] = feeds[:, :, at : at + tall]
    down[...] = feeds[:, :, 5 * piece : 5 * piece + tall]


def deliver(reps, keep, other):
    quota = NAD // 2
    shape = lambda *dims: jax.ShapeDtypeStruct(dims, f32)
    return pl.pallas_call(
        functools.partial(deliver_kernel, reps),
        out_shape=[
            shape(6, quota, R, D // reps),
            shape(quota, R, FF // reps),
            shape(3, quota, R, D // reps),
            shape(2, quota, R, KV // reps),
            shape(2, quota, R, FF // reps),
        ],
        in_specs=[VMEM] * 2,
        out_specs=[VMEM] * 5,
        scratch_shapes=[
            pltpu.VMEM((quota, R, feed_lanes(reps)), f32),
            pltpu.VMEM((quota, R, qkv_lanes(reps)), f32),
        ],
        compiler_params=pltpu.CompilerParams(vmem_limit_bytes=8 << 20),
        cost_estimate=pl.CostEstimate(flops=10**6, bytes_accessed=1 << 20, transcendentals=0),
        name="deliver",
    )(keep, other)


def per_device(
    tokens,
    cotangent,
    segment_ids,
    adapter_ids,
    norm_gains,
    frozen_qkv,
    frozen_out,
    frozen_gate_up,
    frozen_down,
    lower_mats,
    lower_down,
    upper_width,
    upper_keys,
    upper_hidden,
):
    reps = lax.axis_size("rep")
    chosen = adapter_ids[0]
    first = lax.axis_index("grp") == 0
    swap = lambda value: lax.ppermute(value, "grp", SWAP)

    tok_own = tokens[0]
    tok_oth = swap(tok_own)
    qkv_oth = swap(frozen_qkv)
    gains_oth = swap(norm_gains)
    a_down = jnp.pad(
        lax.dynamic_index_in_dim(lower_down, chosen, 0, keepdims=False), ((0, 0), (0, 128 - R))
    )
    tok_oth, qkv_oth, gains_oth, a_down, wo, wgu, wd = lax.optimization_barrier(
        (tok_oth, qkv_oth, gains_oth, a_down, frozen_out, frozen_gate_up, frozen_down)
    )
    wo_oth = swap(wo)
    wgu_oth = swap(wgu)
    wd_oth = swap(wd)

    lower_t = lower_mats.transpose(0, 1, 3, 2)
    gains = (norm_gains, gains_oth)

    (o_own, o_send, query, key_t, value_t, mixed_t, normed, zt, lse, cosine, sine) = attend(
        adapter_ids,
        tok_own,
        tok_oth,
        frozen_qkv,
        qkv_oth,
        lower_t,
        upper_width,
        upper_keys,
        *gains,
        segment_ids,
    )
    o_oth = swap(o_send)
    layer_out, grad_middle, do_own, do_send, pack_own, pack_send = feed(
        reps,
        adapter_ids,
        o_own,
        o_oth,
        tok_own,
        cotangent[0],
        frozen_out,
        wo_oth,
        frozen_gate_up,
        wgu_oth,
        frozen_down,
        wd_oth,
        a_down,
        lower_t,
        upper_width,
        upper_hidden,
        *gains,
    )
    do_oth = swap(do_send)
    pack_oth = swap(pack_send)
    dy, dz, part_send, exchange = attend_back(
        reps,
        adapter_ids,
        do_own,
        do_oth,
        mixed_t,
        normed,
        frozen_qkv,
        qkv_oth,
        lower_t,
        upper_width,
        upper_keys,
        query,
        key_t,
        value_t,
        zt,
        lse,
        cosine,
        sine,
        segment_ids,
        pack_own,
        pack_oth,
    )
    received = lax.all_to_all(exchange, "rep", 0, 0, tiled=True)
    input_grad = finish(
        adapter_ids,
        dy,
        dz,
        frozen_qkv,
        qkv_oth,
        lower_t,
        tok_own,
        *gains,
        swap(part_send),
        grad_middle,
    )
    received, input_grad = lax.optimization_barrier((received, input_grad))
    keep, send = collect(received)
    lower, down, width, keys, hidden = deliver(reps, keep, swap(send))
    return (
        layer_out[None],
        input_grad[None],
        lower.transpose(0, 1, 3, 2),
        down.transpose(0, 2, 1),
        width,
        keys,
        hidden,
    )


def solution(mesh):
    return jax.shard_map(
        per_device,
        mesh=mesh,
        in_specs=(
            P("rep", "grp", None),
            P("rep", "grp", None),
            P("rep", None),
            P("rep"),
            P(None, "grp"),
            P("grp", None),
            P("grp", None),
            P("grp", None),
            P("grp", None),
            P(),
            P(),
            P(),
            P(),
            P(),
        ),
        out_specs=(
            P("rep", "grp", None),
            P("rep", "grp", None),
            P(None, "grp", "rep", None),
            P("grp", "rep", None),
            P(None, "grp", None, "rep"),
            P(None, "grp", None, "rep"),
            P(None, "grp", None, "rep"),
        ),
        check_vma=False,
    )
```

profile of v0, /device:TPU:0, one launch (start us, length us, event | category | flops | bytes accessed | tf_op | source)
XLA Modules:
  0.0 131.3 jit_solution(16268290606036185294)
XLA Ops:
  0.6 0.0 copy-start
  0.6 0.0 copy-start.1
  0.7 0.5 collective-permute-start.1
  1.2 0.1 collective-permute-start
  1.3 0.4 collective-permute-start.2
  2.3 0.0 copy-done
  2.4 0.4 copy.21
  2.8 1.0 pad.4.a_down
  3.8 1.5 %collective-permute-done.2.gains_oth = bf16[2,576]{1,0:T(2,128)(2,1)S(1)} collective-permute-done((bf16[2,576]{1,0:T(2,128)(2,1)}, bf16[2,576]{1,0:T(2,128)(2,1)S(1)}, u32[]{:S(2)}, u32[]{:S(2)}) %collective-permute-start.2) | collective-permute-done | bytes 2336 | tf_op jit(solution)/shard_map/ppermute | solution.py:1166
  5.3 0.0 copy-start.6
  5.3 1.8 %collective-permute-done.tok_oth = bf16[512,1152]{1,0:T(8,128)(2,1)} collective-permute-done((bf16[512,1152]{1,0:T(8,128)(2,1)}, bf16[512,1152]{1,0:T(8,128)(2,1)}, u32[]{:S(2)}, u32[]{:S(2)}) %collective-permute-start) | collective-permute-done | bytes 1179680 | tf_op jit(solution)/shard_map/ppermute | solution.py:1166
  7.2 0.0 collective-permute-done.1.qkv_oth
  7.2 0.4 collective-permute-start.5
  7.5 0.1 collective-permute-start.6
  7.7 0.0 copy-done.1
  7.7 0.4 collective-permute-start.4
  8.1 0.0 copy-done.6
  8.1 21.2 %attend.1 = (bf16[512,640]{1,0:T(8,128)(2,1)}, bf16[512,640]{1,0:T(8,128)(2,1)}, bf16[640,1024]{1,0:T(8,128)(2,1)}, bf16[256,1024]{1,0:T(8,128)(2,1)}, bf16[256,...) custom-call(s32[1]{0:T(128)} %copy.22.adapter, ...), custom_call_target="tpu_custom_call" | custom-call | flops 16000000000 | bytes 16777216 | tf_op jit(solution)/shard_map/attend/pallas_call | solution.py:352
  29.3 0.2 collective-permute-start.3
  29.5 2.2 %collective-permute-done.3.o_oth_in = bf16[512,640]{1,0:T(8,128)(2,1)S(1)} collective-permute-done((bf16[512,640]{1,0:T(8,128)(2,1)}, bf16[512,640]{1,0:T(8,128)(2,1)S(1)}, u32[]{:S(2)}, u32[]{:S(2)}) %collective-permute-start.3) | collective-permute-done | bytes 655392 | tf_op jit(solution)/shard_map/ppermute | solution.py:1166
  31.6 0.0 copy-start.4
  31.6 0.0 collective-permute-done.4.wo_oth
  31.7 0.0 collective-permute-done.6.wd_oth
  31.7 0.0 collective-permute-done.5.wgu_oth
  31.7 0.8 copy-done.4
  32.5 41.7 %feed.1 = (bf16[512,1152]{1,0:T(8,128)(2,1)}, f32[512,1152]{1,0:T(8,128)}, bf16[640,512]{1,0:T(8,128)(2,1)}, bf16[640,512]{1,0:T(8,128)(2,1)}, bf16[256,512]{1,0:T(8,128)(2,1)}, /*index=5*/bf16[256,512]{1,0:T(8,128)(2,1)}) custom-call(s32[1]{0:T(128)} %copy.22.adapter, bf16[512,640]{1,0:T(8,128)(2,1)} %get-tuple-element.47.o_own_in, ...), custom_call_target="tpu_custom_call" | custom-call | flops 30000001024 | bytes 37748736 | tf_op jit(solution)/shard_map/feed/pallas_call | solution.py:660
  74.2 0.2 collective-permute-start.7
  74.4 0.4 collective-permute-start.8
  74.8 2.2 %collective-permute-done.8.pack_oth_in = bf16[256,512]{1,0:T(8,128)(2,1)S(1)} collective-permute-done((bf16[256,512]{1,0:T(8,128)(2,1)}, bf16[256,512]{1,0:T(8,128)(2,1)S(1)}, u32[]{:S(2)}, u32[]{:S(2)}) %collective-permute-start.8) | collective-permute-done | bytes 262176 | tf_op jit(solution)/shard_map/ppermute | solution.py:1166
  76.9 0.0 copy-start.5
  76.9 0.0 collective-permute-done.7.do_oth
  76.9 0.0 copy-start.3
  76.9 0.7 copy-done.5
  77.7 0.3 copy-done.3
  77.9 27.7 %attend_back.1 = (bf16[512,1152]{1,0:T(8,128)(2,1)}, bf16[512,128]{1,0:T(8,128)(2,1)}, bf16[512,1152]{1,0:T(8,128)(2,1)}, bf16[256,896]{1,0:T(8,128)(2,1)}) custom-call(s32[1]{0:T(128)} %copy.22.adapter, bf16[640,512]{1,0:T(8,128)(2,1)} %get-tuple-element.54.do_own, bf16[640,512]{1,0:T(8,128)(2,1)} %copy-done.3, bf16[704,1024]{1,0:T(8,128)(2,1)} %get-tuple-element.56.o_in, ...), custom_call_target="tpu_custom_call" | custom-call | flops 24000000000 | bytes 20971520 | tf_op jit(solution)/shard_map/attend_back/pallas_call | solution.py:925
  105.6 0.2 collective-permute-start.9
  105.8 8.2 %all-to-all-start = ((bf16[16,16,896]{2,1,0:T(8,128)(2,1)}), bf16[16,16,896]{2,1,0:T(8,128)(2,1)S(1)}, u32[]{:S(2)}, u32[]{:S(2)}) async-start(bf16[16,16,896]{2,1,0:T(8,128)(2,1)} %bitcast.16), calls=%async_computation | async-start | bytes 917504 | tf_op jit(solution)/shard_map/all_to_all | solution.py:1242
  114.0 0.0 collective-permute-done.9.part_in
  114.0 0.0 copy-start.2
  114.1 1.0 copy-done.2
  115.1 8.3 %finish.1 = bf16[512,1152]{1,0:T(8,128)(2,1)} custom-call(s32[1]{0:T(128)} %copy.22.adapter, bf16[512,1152]{1,0:T(8,128)(2,1)} %get-tuple-element.68.dy_in, bf16[512,128]{1,0:T(8,128)(2,1)} %get-tuple-element.69.dz_in, bf16[576,1920]{1,0:T(8,128)(2,1)} %qkv_own.5, bf16[576,1920]{1,0:T(8,128)(2,1)} %collective-permute-done.1.qkv_oth, ...), custom_call_target="tpu_custom_call" | custom-call | flops 4000000000 | bytes 10485760 | tf_op jit(solution)/shard_map/finish/pallas_call | solution.py:1039
  123.4 4.8 %all-to-all-done = bf16[16,16,896]{2,1,0:T(8,128)(2,1)S(1)} async-done(((bf16[16,16,896]{2,1,0:T(8,128)(2,1)}), bf16[16,16,896]{2,1,0:T(8,128)(2,1)S(1)}, u32[]{:S(2)}, u32[]{:S(2)}) %all-to-all-start) | async-done | bytes 458784 | tf_op jit(solution)/shard_map/all_to_all | solution.py:1242
  128.2 0.6 collect.1
  128.8 0.1 collective-permute-start.10
  128.9 1.5 %collective-permute-done.10.other = f32[4,16,896]{2,1,0:T(8,128)S(1)} collective-permute-done((f32[4,16,896]{2,1,0:T(8,128)S(1)}, f32[4,16,896]{2,1,0:T(8,128)S(1)}, u32[]{:S(2)}, u32[]{:S(2)}) %collective-permute-start.10) | collective-permute-done | bytes 229408 | tf_op jit(solution)/shard_map/ppermute | solution.py:1166
  130.4 1.0 deliver.1
  (1 shorter events, 0.0 us)
Async XLA Ops:
  0.6 1.7 %copy-start = (bf16[8,3072,16]{1,2,0:T(8,128)(2,1)S(1)}, bf16[8,3072,16]{1,2,0:T(8,128)(2,1)}, u32[]{:S(2)}) copy-start(bf16[8,3072,16]{1,2,0:T(8,128)(2,1)} %param.24) | copy-start | bytes 2359300
  0.6 7.0 %copy-start.1 = (bf16[576,1152]{1,0:T(8,128)(2,1)S(1)}, bf16[576,1152]{1,0:T(8,128)(2,1)}, u32[]{:S(2)}) copy-start(bf16[576,1152]{1,0:T(8,128)(2,1)} %wo_own.1) | copy-start | bytes 3981316
  0.7 6.5 %collective-permute-start.1 = (bf16[576,1920]{1,0:T(8,128)(2,1)}, bf16[576,1920]{1,0:T(8,128)(2,1)}, u32[]{:S(2)}, u32[]{:S(2)}) collective-permute-start(bf16[576,1920]{1,0:T(8,128)(2,1)} %qkv_own.5), channel_id=1, source_target_pairs={{0,16},{16,0},{1,17},{17,1},{2,18},{18,2},{3,19},{19,3},{4,20},{20... | collective-permute-start | bytes 6635528 | tf_op jit(solution)/shard_map/ppermute | solution.py:1166
  1.2 6.0 %collective-permute-start = (bf16[512,1152]{1,0:T(8,128)(2,1)}, bf16[512,1152]{1,0:T(8,128)(2,1)}, u32[]{:S(2)}, u32[]{:S(2)}) collective-permute-start(bf16[512,1152]{1,0:T(8,128)(2,1)} %bitcast.22), channel_id=1, source_target_pairs={{0,16},{16,0},{1,17},{17,1},{2,18},{18,2},{3,19},{19,3},{4,20},{20... | collective-permute-start | bytes 3538952 | tf_op jit(solution)/shard_map/ppermute | solution.py:1166
  1.3 4.1 %collective-permute-start.2 = (bf16[2,576]{1,0:T(2,128)(2,1)}, bf16[2,576]{1,0:T(2,128)(2,1)S(1)}, u32[]{:S(2)}, u32[]{:S(2)}) collective-permute-start(bf16[2,576]{1,0:T(2,128)(2,1)} %gains_own.5), channel_id=1, source_target_pairs={{0,16},{16,0},{1,17},{17,1},{2,18},{18,2},{3,19},{19,3},{4,20},{20... | collective-permute-start | bytes 6920 | tf_op jit(solution)/shard_map/ppermute | solution.py:1166
  5.3 2.7 %copy-start.6 = (bf16[2,576]{1,0:T(2,128)(2,1)}, bf16[2,576]{1,0:T(2,128)(2,1)S(1)}, u32[]{:S(2)}) copy-start(bf16[2,576]{1,0:T(2,128)(2,1)S(1)} %collective-permute-done.2.gains_oth) | copy-start | bytes 6916
  7.2 24.5 %collective-permute-start.5 = (bf16[576,6144]{1,0:T(8,128)(2,1)}, bf16[576,6144]{1,0:T(8,128)(2,1)}, u32[]{:S(2)}, u32[]{:S(2)}) collective-permute-start(bf16[576,6144]{1,0:T(8,128)(2,1)} %wgu_own.1), channel_id=1, source_target_pairs={{0,16},{16,0},{1,17},{17,1},{2,18},{18,2},{3,19},{19,3},{4,20},{20... | collective-permute-start | bytes 21233672 | tf_op jit(solution)/shard_map/ppermute | solution.py:1166
  7.5 24.1 %collective-permute-start.6 = (bf16[1536,1152]{1,0:T(8,128)(2,1)}, bf16[1536,1152]{1,0:T(8,128)(2,1)}, u32[]{:S(2)}, u32[]{:S(2)}) collective-permute-start(bf16[1536,1152]{1,0:T(8,128)(2,1)} %wd_own.1), channel_id=1, source_target_pairs={{0,16},{16,0},{1,17},{17,1},{2,18},{18,2},{3,19},{19,3},{4,20},{20... | collective-permute-start | bytes 10616840 | tf_op jit(solution)/shard_map/ppermute | solution.py:1166
  7.7 24.0 %collective-permute-start.4 = (bf16[576,1152]{1,0:T(8,128)(2,1)S(1)}, bf16[576,1152]{1,0:T(8,128)(2,1)}, u32[]{:S(2)}, u32[]{:S(2)}) collective-permute-start(bf16[576,1152]{1,0:T(8,128)(2,1)S(1)} %copy-done.1), channel_id=1, source_target_pairs={{0,16},{16,0},{1,17},{17,1},{2,18},{18,2},{3,19},{19,3},{4,20},{20... | collective-permute-start | bytes 3981320 | tf_op jit(solution)/shard_map/ppermute | solution.py:1166
  29.3 2.4 %collective-permute-start.3 = (bf16[512,640]{1,0:T(8,128)(2,1)}, bf16[512,640]{1,0:T(8,128)(2,1)S(1)}, u32[]{:S(2)}, u32[]{:S(2)}) collective-permute-start(bf16[512,640]{1,0:T(8,128)(2,1)} %get-tuple-element.48), channel_id=1, source_target_pairs={{0,16},{16,0},{1,17},{17,1},{2,18},{18,2},{3,19},{19,3},{4,20},{20... | collective-permute-start | bytes 1966088 | tf_op jit(solution)/shard_map/ppermute | solution.py:1166
  31.6 0.8 copy-start.4
  74.2 2.8 %collective-permute-start.7 = (bf16[640,512]{1,0:T(8,128)(2,1)}, bf16[640,512]{1,0:T(8,128)(2,1)S(1)}, u32[]{:S(2)}, u32[]{:S(2)}) collective-permute-start(bf16[640,512]{1,0:T(8,128)(2,1)} %get-tuple-element.55), channel_id=1, source_target_pairs={{0,16},{16,0},{1,17},{17,1},{2,18},{18,2},{3,19},{19,3},{4,20},{20... | collective-permute-start | bytes 1966088 | tf_op jit(solution)/shard_map/ppermute | solution.py:1166
  74.4 2.6 %collective-permute-start.8 = (bf16[256,512]{1,0:T(8,128)(2,1)}, bf16[256,512]{1,0:T(8,128)(2,1)S(1)}, u32[]{:S(2)}, u32[]{:S(2)}) collective-permute-start(bf16[256,512]{1,0:T(8,128)(2,1)} %get-tuple-element.66), channel_id=1, source_target_pairs={{0,16},{16,0},{1,17},{17,1},{2,18},{18,2},{3,19},{19,3},{4,20},{20... | collective-permute-start | bytes 786440 | tf_op jit(solution)/shard_map/ppermute | solution.py:1166
  76.9 0.7 copy-start.5
  76.9 1.0 copy-start.3
  105.6 8.4 %collective-permute-start.9 = (bf16[512,1152]{1,0:T(8,128)(2,1)}, bf16[512,1152]{1,0:T(8,128)(2,1)S(1)}, u32[]{:S(2)}, u32[]{:S(2)}) collective-permute-start(bf16[512,1152]{1,0:T(8,128)(2,1)} %get-tuple-element.70), channel_id=1, source_target_pairs={{0,16},{16,0},{1,17},{17,1},{2,18},{18,2},{3,19},{19,3},{4,20},{20... | collective-permute-start | bytes 3538952 | tf_op jit(solution)/shard_map/ppermute | solution.py:1166
  105.8 22.4 %all-to-all-start = ((bf16[16,16,896]{2,1,0:T(8,128)(2,1)}), bf16[16,16,896]{2,1,0:T(8,128)(2,1)S(1)}, u32[]{:S(2)}, u32[]{:S(2)}) async-start(bf16[16,16,896]{2,1,0:T(8,128)(2,1)} %bitcast.16), calls=%async_computation | async-start | bytes 917504 | tf_op jit(solution)/shard_map/all_to_all | solution.py:1242
  114.0 1.0 copy-start.2
  128.8 1.6 %collective-permute-start.10 = (f32[4,16,896]{2,1,0:T(8,128)S(1)}, f32[4,16,896]{2,1,0:T(8,128)S(1)}, u32[]{:S(2)}, u32[]{:S(2)}) collective-permute-start(f32[4,16,896]{2,1,0:T(8,128)S(1)} %get-tuple-element.75), channel_id=1, source_target_pairs={{0,16},{16,0},{1,17},{17,1},{2,18},{18,2},{3,19},{19,3},{4,20},{20... | collective-permute-start | bytes 688136 | tf_op jit(solution)/shard_map/ppermute | solution.py:1166
where the time goes:
time: 132 us; the launch traced here: 131 us
  Pallas kernels  100 us (76%)
  waiting for transfers between devices  14 us (11%)
  starting transfers between devices  11.2 us (8%)
  local copies, waits for them, and re-layouts  4.31 us (3%)
  between operations  1.42 us (1%)
    pallas_call x1, Pallas kernels, feed(): pl.pallas_call(functools.partial(feed_kernel, reps), out_shape=[shape((ro...  41.7 us
    pallas_call x1, Pallas kernels, attend_back(): pl.pallas_call(functools.partial(attend_back_kernel, reps), out_shape=[sh...  27.7 us
    pallas_call x1, Pallas kernels, attend(): pl.pallas_call(attend_kernel, out_shape=[shape((rows, QW), bf16), shape((...  21.2 us
    ppermute x11, waiting for transfers between devices, per_device(): swap = lambda value: lax.ppermute(value, 'grp', SWAP)  9.21 us
    pallas_call x1, Pallas kernels, finish(): pl.pallas_call(finish_kernel, out_shape=jax.ShapeDtypeStruct((rows, D), b...  8.33 us
    all_to_all x1, starting transfers between devices, per_device(): received = lax.all_to_all(exchange, 'rep', 0, 0, tiled=True)  8.23 us
    all_to_all x1, waiting for transfers between devices, per_device(): received = lax.all_to_all(exchange, 'rep', 0, 0, tiled=True)  4.76 us
    ppermute x11, starting transfers between devices, per_device(): swap = lambda value: lax.ppermute(value, 'grp', SWAP)  2.95 us
  transfers between devices with their start and end apart: 12, of which 6 were waited for; matrix products, arithmetic and copies ran while one was open for 1% of the time, Pallas kernels for 22%

commit v1 on v0

--- a/solution.py
+++ b/solution.py
@@ -24,8 +24,9 @@
 KW = 256
 SPAN = QW + 2 * KW
 AUG = D + 128
-TILE = 512
+TILE = 768
 BLOCK = 256
+BLOCKS = 1024 // BLOCK
 DOCS = 4
 KEYS = HEADS // GROUP
 VMEM_BYTES = 61900 * 1024
@@ -193,9 +194,65 @@
     o_out,
     n_out,
     zt_out,
-    lse_out,
+    scale_out,
     cos_out,
     sin_out,
+    *refs,
+):
+    attend_body(
+        adapter,
+        tok_own,
+        tok_oth,
+        qkv_own,
+        qkv_oth,
+        lower_t,
+        upper_width,
+        upper_keys,
+        gains_own,
+        gains_oth,
+        segments,
+        o_own,
+        o_send,
+        q_out,
+        k_out,
+        v_out,
+        o_out,
+        n_out,
+        zt_out,
+        scale_out,
+        cos_out,
+        sin_out,
+        refs[:BLOCKS],
+        refs[BLOCKS : 2 * BLOCKS],
+        *refs[2 * BLOCKS :],
+    )
+
+
+def attend_body(
+    adapter,
+    tok_own,
+    tok_oth,
+    qkv_own,
+    qkv_oth,
+    lower_t,
+    upper_width,
+    upper_keys,
+    gains_own,
+    gains_oth,
+    segments,
+    o_own,
+    o_send,
+    q_out,
+    k_out,
+    v_out,
+    o_out,
+    n_out,
+    zt_out,
+    scale_out,
+    cos_out,
+    sin_out,
+    chances_out,
+    chances,
     tok,
     normed,
     weight,
@@ -208,15 +265,15 @@
     mixed_t,
     mixed,
     scores,
-    chances,
     bias,
     cosine,
     sine,
     inner_t,
-    lse,
+    scales,
     sems,
     w_sems,
     out_sems,
+    keep_sem,
 ):
     g = lax.axis_index("grp")
     chosen = adapter[0]
@@ -295,8 +352,9 @@
     mixed_t[:HD, :] = jnp.zeros((HD, 2 * rows), bf16)
     mixed_t[(HEADS + 1) * HD :, :] = jnp.zeros((HD, 2 * rows), bf16)
 
-    for block in range(2 * rows // BLOCK):
+    for block in reversed(range(BLOCKS)):
         low, high = block * BLOCK, (block + 1) * BLOCK
+        kept = chances[block]
         fill_mask(bias, starts, low, high)
 
         def score(h, side, low=low, high=high):
@@ -312,14 +370,14 @@
                 top = best if top is None else jnp.maximum(top, best)
             return jnp.max(top, axis=0, keepdims=True)
 
-        def blend(h, side, top, low=low, high=high):
+        def blend(h, side, top, low=low, high=high, kept=kept):
             for first in range(0, high, BLOCK):
                 span = slice(first, first + BLOCK)
-                chances[side, span, :] = jnp.exp(scores[side, span, :] - top).astype(bf16)
-            made = nn(value_aug[h // GROUP, :, :high], chances[side, :high, :])
-            total = made[HD : HD + 1]
-            mixed_t[head_rows(h + 1), low:high] = (made[:HD] * (1.0 / total)).astype(bf16)
-            lse[pl.ds(h, 1), low:high] = top + jnp.log(total)
+                kept[h, span, :] = jnp.exp(scores[side, span, :] - top).astype(bf16)
+            made = nn(value_aug[h // GROUP, :, :high], kept[h])
+            scale = 1.0 / made[HD : HD + 1]
+            mixed_t[head_rows(h + 1), low:high] = (made[:HD] * scale).astype(bf16)
+            scales[pl.ds(h, 1), low:high] = scale
 
         def group(j, top, score=score, blend=blend):
             for member in range(GROUP):
@@ -330,18 +388,20 @@
             return top
 
         lax.fori_loop(0, KEYS, group, score(0, 0))
+        stores.append(copied(kept, chances_out[block], keep_sem.at[block]))
+        stores[-1].start()
         for pair in range(QW // 128):
             side = pl.ds(pl.multiple_of((2 * pair + 1 - g) * HD, HD), 128)
             mixed[low:high, pair * 128 : pair * 128 + 128] = mixed_t[side, low:high].T
-    stores += [
+    last = [
         copied(mixed.at[here], o_own, out_sems.at[7]),
         copied(mixed.at[there], o_send, out_sems.at[8]),
         copied(mixed_t, o_out, out_sems.at[9]),
-        copied(lse, lse_out, out_sems.at[10]),
+        copied(scales, scale_out, out_sems.at[10]),
     ]
-    for store in stores[-4:]:
+    for store in last:
         store.start()
-    for store in stores:
+    for store in stores + last:
         store.wait()
 
 
@@ -363,10 +423,14 @@
             shape((R, length), f32),
             shape((HD // 2, length), f32),
             shape((HD // 2, length), f32),
-        ],
+        ]
+        + [shape((HEADS, (block + 1) * BLOCK, BLOCK), bf16) for block in range(BLOCKS)],
         in_specs=[SMEM, HBM, ANY, HBM, ANY] + [HBM] * 3 + [VMEM] * 3,
-        out_specs=[HBM] * 11,
+        out_specs=[HBM] * (11 + BLOCKS),
         scratch_shapes=[
+            pltpu.VMEM((HEADS, (block + 1) * BLOCK, BLOCK), bf16) for block in range(BLOCKS)
+        ]
+        + [
             pltpu.VMEM((length, D), bf16),
             pltpu.VMEM((length, AUG), bf16),
             pltpu.VMEM((AUG, SPAN), bf16),
@@ -379,7 +443,6 @@
             pltpu.VMEM(((HEADS + 2) * HD, length), bf16),
             pltpu.VMEM((length, QW), bf16),
             pltpu.VMEM((GROUP, length, BLOCK), f32),
-            pltpu.VMEM((GROUP, length, BLOCK), bf16),
             pltpu.VMEM((length, BLOCK), f32),
             pltpu.VMEM((HD // 2, length), f32),
             pltpu.VMEM((HD // 2, length), f32),
@@ -388,8 +451,9 @@
             pltpu.SemaphoreType.DMA((5,)),
             pltpu.SemaphoreType.DMA((9,)),
             pltpu.SemaphoreType.DMA((11,)),
+            pltpu.SemaphoreType.DMA((BLOCKS,)),
         ],
-        compiler_params=pltpu.CompilerParams(vmem_limit_bytes=VMEM_BYTES),
+        compiler_params=pltpu.CompilerParams(vmem_limit_bytes=50 << 20),
         cost_estimate=pl.CostEstimate(
             flops=16 * 10**9, bytes_accessed=16 << 20, transcendentals=6 * 10**6
         ),
@@ -474,9 +538,6 @@
     z_gu_t,
     dz_down_t,
     ga_out,
-    gb_gate,
-    gb_up,
-    ga_down,
     pack,
     sems,
     o_sems,
@@ -563,6 +624,7 @@
     first, second, third = loads[11:] + loads[2:4] + loads[7:8], loads[:2] + loads[8:10], loads[4:7] + loads[10:11]
     for load in first + second + third:
         load.start()
+    pack[...] = jnp.zeros_like(pack)
     total[...] = jnp.zeros_like(total)
     back[...] = jnp.zeros_like(back)
     for load in first:
@@ -593,7 +655,6 @@
             start(step + 1, 1 - slot)
 
         wait(step, slot)
-        gate_at = pl.ds(pl.multiple_of(column(step), TILE), TILE)
         gate = nn(normed[...], wg[slot])
         up = nn(normed[...], wu[slot])
         grad_active = nt(cot_aug[...], wd[slot])
@@ -604,9 +665,18 @@
         grad_up = (grad_active * silu).astype(bf16)
         total[...] += nn(active, wd[slot])
         back[...] += nt(grad_gate, wg[slot]) + nt(grad_up, wu[slot])
-        gb_gate[:, gate_at] = nn(z_gu_t[...], grad_gate)[:R]
-        gb_up[:, gate_at] = nn(z_gu_t[...], grad_up)[R:]
-        ga_down[:, gate_at] = nn(dz_down_t[...], active)
+        shares = (
+            nn(dz_down_t[...], active),
+            nn(z_gu_t[...], grad_gate)[:R],
+            nn(z_gu_t[...], grad_up)[R:],
+        )
+        piece = FF // reps
+        base = column(step) // piece
+        for index, share in enumerate(shares):
+            at = 5 * (D // reps) + index * piece
+            for rep in range(TILE // piece):
+                target = pl.ds(pl.multiple_of((base + rep) * R, R), R)
+                pack[target, at : at + piece] = share[:, rep * piece : (rep + 1) * piece].astype(bf16)
         return carry
 
     lax.fori_loop(0, steps, step_body, 0)
@@ -638,12 +708,7 @@
     ga_out[...] = jnp.zeros_like(ga_out)
     ga_out[:, pl.ds(own_at, QW)] += nn(dz_out_t, o_own[...])
     ga_out[:, pl.ds(oth_at, QW)] += nn(dz_out_t, o_oth[...])
-    pack[...] = jnp.zeros_like(pack)
-    packed(
-        [ga_out[...], ga_gu[:R], ga_gu[R:], gb_out, gb_down, ga_down[...], gb_gate[...], gb_up[...]],
-        reps,
-        pack,
-    )
+    packed([ga_out[...], ga_gu[:R], ga_gu[R:], gb_out, gb_down], reps, pack)
     half = pack.shape[1] // 2
     for index, (side, target) in enumerate(((g, pack_own_out), (1 - g, pack_send_out))):
         source = pack.at[:, pl.ds(pl.multiple_of(side * half, 128), half)]
@@ -693,15 +758,12 @@
             pltpu.VMEM((2 * R, rows), bf16),
             pltpu.VMEM((R, rows), bf16),
             pltpu.VMEM((R, D), f32),
-            pltpu.VMEM((R, FF), f32),
-            pltpu.VMEM((R, FF), f32),
-            pltpu.VMEM((R, FF), f32),
             pltpu.VMEM((reps * R, 2 * half), bf16),
             pltpu.SemaphoreType.DMA((2, 8)),
             pltpu.SemaphoreType.DMA((12,)),
             pltpu.SemaphoreType.DMA((6,)),
         ],
-        compiler_params=pltpu.CompilerParams(vmem_limit_bytes=56 << 20),
+        compiler_params=pltpu.CompilerParams(vmem_limit_bytes=46 << 20),
         cost_estimate=pl.CostEstimate(
             flops=30 * 10**9, bytes_accessed=36 << 20, transcendentals=2 * 10**6
         ),
@@ -725,12 +787,64 @@
     k_in,
     v_in,
     zt_in,
-    lse_in,
+    scale_in,
     cos_in,
     sin_in,
-    segments,
     pack_own_in,
     pack_oth_in,
+    *refs,
+):
+    attend_back_body(
+        reps,
+        adapter,
+        do_own,
+        do_oth,
+        o_in,
+        normed,
+        qkv_own,
+        qkv_oth,
+        lower_t,
+        upper_width,
+        upper_keys,
+        query_in,
+        k_in,
+        v_in,
+        zt_in,
+        scale_in,
+        cos_in,
+        sin_in,
+        pack_own_in,
+        pack_oth_in,
+        refs[:BLOCKS],
+        refs[BLOCKS + 4 : 2 * BLOCKS + 4],
+        *refs[BLOCKS : BLOCKS + 4],
+        *refs[2 * BLOCKS + 4 :],
+    )
+
+
+def attend_back_body(
+    reps,
+    adapter,
+    do_own,
+    do_oth,
+    o_in,
+    normed,
+    qkv_own,
+    qkv_oth,
+    lower_t,
+    upper_width,
+    upper_keys,
+    query_in,
+    k_in,
+    v_in,
+    zt_in,
+    scale_in,
+    cos_in,
+    sin_in,
+    pack_own_in,
+    pack_oth_in,
+    chances_in,
+    chances,
     dy_out,
     dz_out,
     part_out,
@@ -739,7 +853,7 @@
     key_t,
     value_t,
     zt,
-    lse,
+    scales,
     cosine,
     sine,
     pack_own,
@@ -752,7 +866,6 @@
     mixed_t,
     n_rows,
     weight,
-    key_rows,
     value_rows,
     delta,
     dq,
@@ -760,15 +873,14 @@
     dv,
     dy_t,
     dy,
-    chances,
     grad_scores,
-    bias,
     gb_q,
     gb_kv,
     pack,
     sems,
     b_sems,
     out_sem,
+    keep_sem,
 ):
     g = lax.axis_index("grp")
     chosen = adapter[0]
@@ -787,7 +899,7 @@
         copied(do_oth, grad_o.at[:, there], sems.at[3]),
         copied(o_in, mixed_t, sems.at[4]),
         copied(query_in, query, sems.at[5]),
-        copied(lse_in, lse, sems.at[6]),
+        copied(scale_in, scales, sems.at[6]),
     ]
     late = [
         copied(cos_in, cosine, sems.at[7]),
@@ -800,59 +912,59 @@
         copied(lower_t.at[index, chosen], maps.at[pl.ds(index * R, R)], sems.at[13 + index])
         for index in range(3)
     ] + qkv_loads(g, chosen, qkv_own, qkv_oth, upper_width, upper_keys, weight, b_sems)
+    kept = [
+        copied(chances_in[block], chances[block], keep_sem.at[block]) for block in range(BLOCKS)
+    ]
     for load in early + loads:
         load.start()
+    kept[0].start()
     dk[...] = jnp.zeros_like(dk)
     dv[...] = jnp.zeros_like(dv)
     dy_t[...] = jnp.zeros_like(dy_t)
-    starts = doc_starts(segments[...])
     for load in early:
         load.wait()
     for j in range(KEYS):
-        key_rows[j] = key_t[head_rows(j + g), :].T
         value_rows[j] = value_t[head_rows(j + g), :].T
     for load in loads:
         load.wait()
-    for load in late:
+    for load in kept[1:] + late:
         load.start()
     for h in range(HEADS):
-        product = grad_o[head_rows(h + g), :].astype(f32) * mixed_t[
-            (h + 1) * HD : (h + 2) * HD, :
-        ].astype(f32)
+        scaled = grad_o[head_rows(h + g), :].astype(f32) * scales[h : h + 1, :]
+        product = scaled * mixed_t[(h + 1) * HD : (h + 2) * HD, :].astype(f32)
         delta[h : h + 1, :] = jnp.sum(product, axis=0, keepdims=True)
+        grad_o[head_rows(h + g), :] = scaled.astype(bf16)
 
     for block in range(length // BLOCK):
         low, high = block * BLOCK, (block + 1) * BLOCK
-        fill_mask(bias, starts, low, high)
-
-        def score(h, side, low=low, high=high):
-            logs = lse[pl.ds(h, 1), low:high]
+        found = chances[block]
+        kept[block].wait()
+
+        def score(h, side, low=low, high=high, found=found):
             deltas = delta[pl.ds(h, 1), low:high]
             for first in range(0, high, BLOCK):
                 span = slice(first, first + BLOCK)
-                made = nn(key_rows[h // GROUP, span, :], query[head_rows(h + g), low:high])
                 grad = nn(value_rows[h // GROUP, span, :], grad_o[head_rows(h + g), low:high])
-                chance = jnp.exp(made + bias[span, :] - logs)
-                chances[side, span, :] = chance.astype(bf16)
+                chance = found[h, span, :].astype(f32)
                 grad_scores[side, span, :] = (chance * (grad - deltas)).astype(bf16)
 
-        def spread(h, side, low=low, high=high):
+        def spread(h, side, low=low, high=high, found=found):
             dq[h, :, low:high] = nn(
                 key_t[head_rows(h // GROUP + g), :high], grad_scores[side, :high, :]
             )
             return (
-                nt(grad_o[head_rows(h + g), low:high], chances[side, :high, :]),
+                nt(grad_o[head_rows(h + g), low:high], found[h]),
                 nt(query[head_rows(h + g), low:high], grad_scores[side, :high, :]),
             )
 
         def group(j, carry, high=high, score=score, spread=spread):
-            found = []
+            sums = []
             for member in range(GROUP):
                 h = j * GROUP + member
                 score(jnp.minimum(h + 1, HEADS - 1), (member + 1) % GROUP)
-                found.append(spread(h, member))
-            dv[j, :, :high] += found[0][0] + found[1][0] + found[2][0]
-            dk[j, :, :high] += found[0][1] + found[1][1] + found[2][1]
+                sums.append(spread(h, member))
+            dv[j, :, :high] += sums[0][0] + sums[1][0] + sums[2][0]
+            dk[j, :, :high] += sums[0][1] + sums[1][1] + sums[2][1]
             return carry
 
         score(0, 0)
@@ -930,9 +1042,12 @@
             shape((rows, D), bf16),
             shape((reps * R, half + width), bf16),
         ],
-        in_specs=[SMEM, HBM, ANY] + [HBM] * 14 + [VMEM, HBM, ANY],
+        in_specs=[SMEM, HBM, ANY] + [HBM] * 15 + [ANY] + [HBM] * BLOCKS,
         out_specs=[HBM] * 4,
         scratch_shapes=[
+            pltpu.VMEM((HEADS, (block + 1) * BLOCK, BLOCK), bf16) for block in range(BLOCKS)
+        ]
+        + [
             pltpu.VMEM((QW, length), bf16),
             pltpu.VMEM((KW, length), bf16),
             pltpu.VMEM((KW, length), bf16),
@@ -951,7 +1066,6 @@
             pltpu.VMEM((length, D), bf16),
             pltpu.VMEM((AUG, SPAN), bf16),
             pltpu.VMEM((KEYS, length, HD), bf16),
-            pltpu.VMEM((KEYS, length, HD), bf16),
             pltpu.VMEM((R, length), f32),
             pltpu.VMEM((HEADS, HD, length), f32),
             pltpu.VMEM((KEYS, HD, length), f32),
@@ -959,16 +1073,15 @@
             pltpu.VMEM(((HEADS + 2 * KEYS + 6) * HD, length), bf16),
             pltpu.VMEM((length, SPAN), bf16),
             pltpu.VMEM((GROUP, length, BLOCK), bf16),
-            pltpu.VMEM((GROUP, length, BLOCK), bf16),
-            pltpu.VMEM((length, BLOCK), f32),
             pltpu.VMEM((R, D), f32),
             pltpu.VMEM((2, R, KV), f32),
             pltpu.VMEM((reps * R, width), bf16),
             pltpu.SemaphoreType.DMA((16,)),
             pltpu.SemaphoreType.DMA((9,)),
             pltpu.SemaphoreType.DMA((4,)),
+            pltpu.SemaphoreType.DMA((BLOCKS,)),
         ],
-        compiler_params=pltpu.CompilerParams(vmem_limit_bytes=56 << 20),
+        compiler_params=pltpu.CompilerParams(vmem_limit_bytes=50 << 20),
         cost_estimate=pl.CostEstimate(
             flops=24 * 10**9, bytes_accessed=20 << 20, transcendentals=6 * 10**6
         ),
@@ -1182,17 +1295,19 @@
     lower_t = lower_mats.transpose(0, 1, 3, 2)
     gains = (norm_gains, gains_oth)
 
-    (o_own, o_send, query, key_t, value_t, mixed_t, normed, zt, lse, cosine, sine) = attend(
-        adapter_ids,
-        tok_own,
-        tok_oth,
-        frozen_qkv,
-        qkv_oth,
-        lower_t,
-        upper_width,
-        upper_keys,
-        *gains,
-        segment_ids,
+    (o_own, o_send, query, key_t, value_t, mixed_t, normed, zt, scales, cosine, sine, *chances) = (
+        attend(
+            adapter_ids,
+            tok_own,
+            tok_oth,
+            frozen_qkv,
+            qkv_oth,
+            lower_t,
+            upper_width,
+            upper_keys,
+            *gains,
+            segment_ids,
+        )
     )
     o_oth = swap(o_send)
     layer_out, grad_middle, do_own, do_send, pack_own, pack_send = feed(
@@ -1232,12 +1347,12 @@
         key_t,
         value_t,
         zt,
-        lse,
+        scales,
         cosine,
         sine,
-        segment_ids,
         pack_own,
         pack_oth,
+        *chances,
     )
     received = lax.all_to_all(exchange, "rep", 0, 0, tiled=True)
     input_grad = finish(

time: 132 us -> 127 us (0.962)
  Pallas kernels: 100 us -> 95.9 us
    pallas_call x1, Pallas kernels: 27.7 us -> 24.3 us  [attend_back(): pl.pallas_call(functools.partial(attend_back_kernel, reps), out_shape=[sh...]
    pallas_call x1, Pallas kernels: 41.7 us -> 40 us  [feed(): pl.pallas_call(functools.partial(feed_kernel, reps), out_shape=[shape((ro...]
    unnamed x14 -> x26, local copies, waits for them, and re-layouts: 2.88 us -> 3.5 us
  transfers between devices with their start and end apart: 12 -> 12, of which waited for: 6 -> 6; matrix products, arithmetic and copies ran while one was open for 1% -> 0% of each run, Pallas kernels for 22% -> 24%
where the time goes in v1:
time: 127 us
  Pallas kernels  95.9 us (76%)
  waiting for transfers between devices  14.3 us (11%)
  starting transfers between devices  11.1 us (9%)
  local copies, waits for them, and re-layouts  4.05 us (3%)
  between operations  1.5 us (1%)
    pallas_call x1, Pallas kernels, feed(): pl.pallas_call(functools.partial(feed_kernel, reps), out_shape=[shape((ro...  40 us
    pallas_call x1, Pallas kernels, attend_back(): pl.pallas_call(functools.partial(attend_back_kernel, reps), out_shape=[sh...  24.3 us
    pallas_call x1, Pallas kernels, attend(): pl.pallas_call(attend_kernel, out_shape=[shape((rows, QW), bf16), shape((...  21.7 us
    ppermute x11, waiting for transfers between devices, per_device(): swap = lambda value: lax.ppermute(value, 'grp', SWAP)  9.64 us
    pallas_call x1, Pallas kernels, finish(): pl.pallas_call(finish_kernel, out_shape=jax.ShapeDtypeStruct((rows, D), b...  8.4 us
    all_to_all x1, starting transfers between devices, per_device(): received = lax.all_to_all(exchange, 'rep', 0, 0, tiled=True)  8.22 us
    all_to_all x1, waiting for transfers between devices, per_device(): received = lax.all_to_all(exchange, 'rep', 0, 0, tiled=True)  4.7 us
    unnamed x26, local copies, waits for them, and re-layouts  3.5 us
  transfers between devices with their start and end apart: 12, of which 6 were waited for; matrix products, arithmetic and copies ran while one was open for 0% of the time, Pallas kernels for 24%

profile of v1, /device:TPU:0, one launch (start us, length us, event | category | flops | bytes accessed | tf_op | source)
XLA Modules:
  0.0 127.0 jit_solution(9856652136264763176)
XLA Ops:
  0.6 0.0 copy-start
  0.7 0.0 copy-start.7
  0.7 0.0 copy-start.4
  0.7 0.0 copy-start.5
  0.7 0.0 copy-start.6
  0.7 0.5 collective-permute-start.1
  1.2 0.1 collective-permute-start
  1.3 0.4 collective-permute-start.2
  2.4 0.0 copy-done
  2.4 0.4 copy.21
  2.8 0.2 pad.4.a_down
  3.0 4.0 %collective-permute-done.2.gains_oth = bf16[2,576]{1,0:T(2,128)(2,1)S(1)} collective-permute-done((bf16[2,576]{1,0:T(2,128)(2,1)}, bf16[2,576]{1,0:T(2,128)(2,1)S(1)}, u32[]{:S(2)}, u32[]{:S(2)}) %collective-permute-start.2) | collective-permute-done | bytes 2336 | tf_op jit(solution)/shard_map/ppermute | solution.py:1279
  7.0 0.0 collective-permute-done.tok_oth
  7.0 0.2 collective-permute-done.1.qkv_oth
  7.2 0.4 collective-permute-start.5
  7.6 0.1 collective-permute-start.6
  7.7 0.4 collective-permute-start.4
  8.1 0.0 copy-done.11
  8.1 0.0 copy-done.5
  8.1 0.0 copy-done.6
  8.1 0.0 copy-start.2
  8.1 0.0 copy-start.3
  8.1 21.7 %attend.1 = (bf16[512,640]{1,0:T(8,128)(2,1)S(1)}, bf16[512,640]{1,0:T(8,128)(2,1)S(1)}, bf16[640,1024]{1,0:T(8,128)(2,1)}, bf16[256,1024]{1,0:T(8,128)(2,1)S(1)...) custom-call(s32[1]{0:T(128)} %copy.22.adapter, ...), custom_call_target="tpu_custom_call" | custom-call | flops 16000000000 | bytes 16777216 | tf_op jit(solution)/shard_map/attend/pallas_call | solution.py:412
  29.8 0.2 collective-permute-start.3
  30.0 1.9 %collective-permute-done.3.o_oth_in = bf16[512,640]{1,0:T(8,128)(2,1)S(1)} collective-permute-done((bf16[512,640]{1,0:T(8,128)(2,1)S(1)}, bf16[512,640]{1,0:T(8,128)(2,1)S(1)}, u32[]{:S(2)}, u32[]{:S(2)}) %collective-permute-start.3) | collective-permute-done | bytes 655392 | tf_op jit(solution)/shard_map/ppermute | solution.py:1279
  32.0 0.0 collective-permute-done.4.wo_oth
  32.0 0.0 collective-permute-done.6.wd_oth
  32.0 0.0 collective-permute-done.5.wgu_oth
  32.0 1.8 %copy-done.10 = bf16[1536,1152]{1,0:T(8,128)(2,1)} copy-done((bf16[1536,1152]{1,0:T(8,128)(2,1)}, bf16[1536,1152]{1,0:T(8,128)(2,1)S(1)}, u32[]{:S(2)}) %copy-start.10) | copy-done | bytes 3538968
  33.8 40.0 %feed.1 = (bf16[512,1152]{1,0:T(8,128)(2,1)}, f32[512,1152]{1,0:T(8,128)}, bf16[640,512]{1,0:T(8,128)(2,1)S(1)}, bf16[640,512]{1,0:T(8,128)(2,1)S(1)}, bf16[256,...) custom-call(s32[1]{0:T(128)} %copy.22.adapter, bf16[512,640]{1,0:T(8,128)(2,1)S(1)} %get-tuple-element.51.o_own_in, ...), custom_call_target="tpu_custom_call" | custom-call | flops 30000001024 | bytes 37748736 | tf_op jit(solution)/shard_map/feed/pallas_call | solution.py:725
  73.8 0.2 collective-permute-start.7
  74.0 0.4 collective-permute-start.8
  74.4 2.0 %collective-permute-done.8.pack_oth_in = bf16[256,512]{1,0:T(8,128)(2,1)S(1)} collective-permute-done((bf16[256,512]{1,0:T(8,128)(2,1)S(1)}, bf16[256,512]{1,0:T(8,128)(2,1)S(1)}, u32[]{:S(2)}, u32[]{:S(2)}) %collective-permute-start.8) | collective-permute-done | bytes 262176 | tf_op jit(solution)/shard_map/ppermute | solution.py:1279
  76.3 0.0 collective-permute-done.7.do_oth
  76.3 24.3 %attend_back.1 = (bf16[512,1152]{1,0:T(8,128)(2,1)}, bf16[512,128]{1,0:T(8,128)(2,1)S(1)}, bf16[512,1152]{1,0:T(8,128)(2,1)}, bf16[256,896]{1,0:T(8,128)(2,1)}) custom-call(s32[1]{0:T(128)} %copy.22.adapter, bf16[640,512]{1,0:T(8,128)(2,1)S(1)} %get-tuple-element.58.do_own, bf16[640,512]{1,0:T(8,128)(2,1)S(1)} %collective-permute-done.7.do_oth, ...), custom_call_target="tpu_custom_call" | custom-call | flops 24000000000 | bytes 20971520 | tf_op jit(solution)/shard_map/attend_back/pallas_call | solution.py:1037
  100.6 0.0 copy-start.9
  100.6 0.6 copy-done.9
  101.3 0.2 collective-permute-start.9
  101.4 8.2 %all-to-all-start = ((bf16[16,16,896]{2,1,0:T(8,128)(2,1)}), bf16[16,16,896]{2,1,0:T(8,128)(2,1)S(1)}, u32[]{:S(2)}, u32[]{:S(2)}) async-start(bf16[16,16,896]{2,1,0:T(8,128)(2,1)} %bitcast.6), calls=%async_computation | async-start | bytes 917504 | tf_op jit(solution)/shard_map/all_to_all | solution.py:1357
  109.7 0.0 collective-permute-done.9.part_in
  109.7 1.0 copy-done.12
  110.7 8.4 %finish.1 = bf16[512,1152]{1,0:T(8,128)(2,1)} custom-call(s32[1]{0:T(128)} %copy.22.adapter, bf16[512,1152]{1,0:T(8,128)(2,1)} %get-tuple-element.76.dy_in, bf16[512,128]{1,0:T(8,128)(2,1)} %copy-done.9, bf16[576,1920]{1,0:T(8,128)(2,1)} %qkv_own.5, bf16[576,1920]{1,0:T(8,128)(2,1)} %collective-permute-done.1.qkv_oth, bf16[6,8,16,1152]{3,2,1,0:T(8,128)(2,1)} %bitcast.24, ...), custom_call_target="tpu_custom_call" | custom-call | flops 4000000000 | bytes 10485760 | tf_op jit(solution)/shard_map/finish/pallas_call | solution.py:1152
  119.1 4.7 %all-to-all-done = bf16[16,16,896]{2,1,0:T(8,128)(2,1)S(1)} async-done(((bf16[16,16,896]{2,1,0:T(8,128)(2,1)}), bf16[16,16,896]{2,1,0:T(8,128)(2,1)S(1)}, u32[]{:S(2)}, u32[]{:S(2)}) %all-to-all-start) | async-done | bytes 458784 | tf_op jit(solution)/shard_map/all_to_all | solution.py:1357
  123.8 0.6 collect.1
  124.4 0.1 collective-permute-start.10
  124.5 1.5 %collective-permute-done.10.other = f32[4,16,896]{2,1,0:T(8,128)S(1)} collective-permute-done((f32[4,16,896]{2,1,0:T(8,128)S(1)}, f32[4,16,896]{2,1,0:T(8,128)S(1)}, u32[]{:S(2)}, u32[]{:S(2)}) %collective-permute-start.10) | collective-permute-done | bytes 229408 | tf_op jit(solution)/shard_map/ppermute | solution.py:1279
  126.0 1.0 deliver.1
  127.0 0.0 copy-done.1
  (11 shorter events, 0.0 us)
Async XLA Ops:
  0.6 1.7 %copy-start = (bf16[8,3072,16]{1,2,0:T(8,128)(2,1)S(1)}, bf16[8,3072,16]{1,2,0:T(8,128)(2,1)}, u32[]{:S(2)}) copy-start(bf16[8,3072,16]{1,2,0:T(8,128)(2,1)} %param.24) | copy-start | bytes 2359300
  0.7 7.4 %copy-start.7 = (bf16[2,576]{1,0:T(2,128)(2,1)S(1)}, bf16[2,576]{1,0:T(2,128)(2,1)}, u32[]{:S(2)}) copy-start(bf16[2,576]{1,0:T(2,128)(2,1)} %gains_own.5) | copy-start | bytes 6916
  0.7 7.4 %copy-start.4 = (bf16[3,8,16,1152]{3,2,1,0:T(8,128)(2,1)S(1)}, bf16[3,8,16,1152]{3,2,1,0:T(8,128)(2,1)}, u32[]{:S(2)}) copy-start(bf16[3,8,16,1152]{3,2,1,0:T(8,128)(2,1)} %upper_width.5) | copy-start | bytes 2654212
  0.7 7.4 %copy-start.5 = (bf16[2,8,16,384]{3,2,1,0:T(8,128)(2,1)S(1)}, bf16[2,8,16,384]{3,2,1,0:T(8,128)(2,1)}, u32[]{:S(2)}) copy-start(bf16[2,8,16,384]{3,2,1,0:T(8,128)(2,1)} %upper_keys.3) | copy-start | bytes 589828
  0.7 7.4 %copy-start.6 = (s32[1,1024]{1,0:T(1,128)S(1)}, s32[1,1024]{1,0:T(1,128)}, u32[]{:S(2)}) copy-start(s32[1,1024]{1,0:T(1,128)} %segments.1) | copy-start | bytes 12292
  0.7 6.5 %collective-permute-start.1 = (bf16[576,1920]{1,0:T(8,128)(2,1)}, bf16[576,1920]{1,0:T(8,128)(2,1)}, u32[]{:S(2)}, u32[]{:S(2)}) collective-permute-start(bf16[576,1920]{1,0:T(8,128)(2,1)} %qkv_own.5), channel_id=1, source_target_pairs={{0,16},{16,0},{1,17},{17,1},{2,18},{18,2},{3,19},{19,3},{4,20},{20... | collective-permute-start | bytes 6635528 | tf_op jit(solution)/shard_map/ppermute | solution.py:1279
  1.2 5.8 %collective-permute-start = (bf16[512,1152]{1,0:T(8,128)(2,1)}, bf16[512,1152]{1,0:T(8,128)(2,1)S(1)}, u32[]{:S(2)}, u32[]{:S(2)}) collective-permute-start(bf16[512,1152]{1,0:T(8,128)(2,1)} %bitcast.16), channel_id=1, source_target_pairs={{0,16},{16,0},{1,17},{17,1},{2,18},{18,2},{3,19},{19,3},{4,20},{20... | collective-permute-start | bytes 3538952 | tf_op jit(solution)/shard_map/ppermute | solution.py:1279
  1.3 5.7 %collective-permute-start.2 = (bf16[2,576]{1,0:T(2,128)(2,1)}, bf16[2,576]{1,0:T(2,128)(2,1)S(1)}, u32[]{:S(2)}, u32[]{:S(2)}) collective-permute-start(bf16[2,576]{1,0:T(2,128)(2,1)} %gains_own.5), channel_id=1, source_target_pairs={{0,16},{16,0},{1,17},{17,1},{2,18},{18,2},{3,19},{19,3},{4,20},{20... | collective-permute-start | bytes 6920 | tf_op jit(solution)/shard_map/ppermute | solution.py:1279
  7.0 25.0 %copy-start.8 = (bf16[2,576]{1,0:T(2,128)(2,1)}, bf16[2,576]{1,0:T(2,128)(2,1)S(1)}, u32[]{:S(2)}) copy-start(bf16[2,576]{1,0:T(2,128)(2,1)S(1)} %collective-permute-done.2.gains_oth) | copy-start | bytes 6916
  7.0 1.1 copy-start.11
  7.2 24.8 %collective-permute-start.5 = (bf16[576,6144]{1,0:T(8,128)(2,1)}, bf16[576,6144]{1,0:T(8,128)(2,1)}, u32[]{:S(2)}, u32[]{:S(2)}) collective-permute-start(bf16[576,6144]{1,0:T(8,128)(2,1)} %wgu_own.1), channel_id=1, source_target_pairs={{0,16},{16,0},{1,17},{17,1},{2,18},{18,2},{3,19},{19,3},{4,20},{20... | collective-permute-start | bytes 21233672 | tf_op jit(solution)/shard_map/ppermute | solution.py:1279
  7.6 24.4 %collective-permute-start.6 = (bf16[1536,1152]{1,0:T(8,128)(2,1)}, bf16[1536,1152]{1,0:T(8,128)(2,1)S(1)}, u32[]{:S(2)}, u32[]{:S(2)}) collective-permute-start(bf16[1536,1152]{1,0:T(8,128)(2,1)} %wd_own.1), channel_id=1, source_target_pairs={{0,16},{16,0},{1,17},{17,1},{2,18},{18,2},{3,19},{19,3},{4,20},{20... | collective-permute-start | bytes 10616840 | tf_op jit(solution)/shard_map/ppermute | solution.py:1279
  7.7 24.3 %collective-permute-start.4 = (bf16[576,1152]{1,0:T(8,128)(2,1)}, bf16[576,1152]{1,0:T(8,128)(2,1)}, u32[]{:S(2)}, u32[]{:S(2)}) collective-permute-start(bf16[576,1152]{1,0:T(8,128)(2,1)} %wo_own.1), channel_id=1, source_target_pairs={{0,16},{16,0},{1,17},{17,1},{2,18},{18,2},{3,19},{19,3},{4,20},{20... | collective-permute-start | bytes 3981320 | tf_op jit(solution)/shard_map/ppermute | solution.py:1279
  8.1 25.7 %copy-start.2 = (bf16[1,512,1152]{2,1,0:T(8,128)(2,1)S(1)}, bf16[1,512,1152]{2,1,0:T(8,128)(2,1)}, u32[]{:S(2)}) copy-start(bf16[1,512,1152]{2,1,0:T(8,128)(2,1)} %param.15) | copy-start | bytes 3538948
  8.1 25.6 %copy-start.3 = (bf16[1,512,1152]{2,1,0:T(8,128)(2,1)S(1)}, bf16[1,512,1152]{2,1,0:T(8,128)(2,1)}, u32[]{:S(2)}) copy-start(bf16[1,512,1152]{2,1,0:T(8,128)(2,1)} %param.14) | copy-start | bytes 3538948
  29.8 2.2 %collective-permute-start.3 = (bf16[512,640]{1,0:T(8,128)(2,1)S(1)}, bf16[512,640]{1,0:T(8,128)(2,1)S(1)}, u32[]{:S(2)}, u32[]{:S(2)}) collective-permute-start(bf16[512,640]{1,0:T(8,128)(2,1)S(1)} %get-tuple-element.52), channel_id=1, source_target_pairs={{0,16},{16,0},{1,17},{17,1},{2,18},{18,2},{3,19},{19,3},{4,20},{20... | collective-permute-start | bytes 1966088 | tf_op jit(solution)/shard_map/ppermute | solution.py:1279
  32.0 1.8 %copy-start.10 = (bf16[1536,1152]{1,0:T(8,128)(2,1)}, bf16[1536,1152]{1,0:T(8,128)(2,1)S(1)}, u32[]{:S(2)}) copy-start(bf16[1536,1152]{1,0:T(8,128)(2,1)S(1)} %collective-permute-done.6.wd_oth) | copy-start | bytes 10616836
  73.8 2.5 %collective-permute-start.7 = (bf16[640,512]{1,0:T(8,128)(2,1)S(1)}, bf16[640,512]{1,0:T(8,128)(2,1)S(1)}, u32[]{:S(2)}, u32[]{:S(2)}) collective-permute-start(bf16[640,512]{1,0:T(8,128)(2,1)S(1)} %get-tuple-element.59), channel_id=1, source_target_pairs={{0,16},{16,0},{1,17},{17,1},{2,18},{18,2},{3,19},{19,3},{4,20},{20... | collective-permute-start | bytes 1966088 | tf_op jit(solution)/shard_map/ppermute | solution.py:1279
  74.0 2.3 %collective-permute-start.8 = (bf16[256,512]{1,0:T(8,128)(2,1)S(1)}, bf16[256,512]{1,0:T(8,128)(2,1)S(1)}, u32[]{:S(2)}, u32[]{:S(2)}) collective-permute-start(bf16[256,512]{1,0:T(8,128)(2,1)S(1)} %get-tuple-element.70), channel_id=1, source_target_pairs={{0,16},{16,0},{1,17},{17,1},{2,18},{18,2},{3,19},{19,3},{4,20},{20... | collective-permute-start | bytes 786440 | tf_op jit(solution)/shard_map/ppermute | solution.py:1279
  100.6 0.7 copy-start.9
  101.3 8.4 %collective-permute-start.9 = (bf16[512,1152]{1,0:T(8,128)(2,1)}, bf16[512,1152]{1,0:T(8,128)(2,1)S(1)}, u32[]{:S(2)}, u32[]{:S(2)}) collective-permute-start(bf16[512,1152]{1,0:T(8,128)(2,1)} %get-tuple-element.78), channel_id=1, source_target_pairs={{0,16},{16,0},{1,17},{17,1},{2,18},{18,2},{3,19},{19,3},{4,20},{20... | collective-permute-start | bytes 3538952 | tf_op jit(solution)/shard_map/ppermute | solution.py:1279
  101.4 22.4 %all-to-all-start = ((bf16[16,16,896]{2,1,0:T(8,128)(2,1)}), bf16[16,16,896]{2,1,0:T(8,128)(2,1)S(1)}, u32[]{:S(2)}, u32[]{:S(2)}) async-start(bf16[16,16,896]{2,1,0:T(8,128)(2,1)} %bitcast.6), calls=%async_computation | async-start | bytes 917504 | tf_op jit(solution)/shard_map/all_to_all | solution.py:1357
  109.7 1.0 copy-start.12
  110.7 16.2 %copy-start.1 = (bf16[8,3072,16]{1,2,0:T(8,128)(2,1)S(1)}, bf16[8,3072,16]{1,2,0:T(8,128)(2,1)}, u32[]{:S(2)}) copy-start(bf16[8,3072,16]{1,2,0:T(8,128)(2,1)} %param.24) | copy-start | bytes 2359300
  124.4 1.6 %collective-permute-start.10 = (f32[4,16,896]{2,1,0:T(8,128)S(1)}, f32[4,16,896]{2,1,0:T(8,128)S(1)}, u32[]{:S(2)}, u32[]{:S(2)}) collective-permute-start(f32[4,16,896]{2,1,0:T(8,128)S(1)} %get-tuple-element.83), channel_id=1, source_target_pairs={{0,16},{16,0},{1,17},{17,1},{2,18},{18,2},{3,19},{19,3},{4,20},{20... | collective-permute-start | bytes 688136 | tf_op jit(solution)/shard_map/ppermute | solution.py:1279

commit v2 on v1

--- a/solution.py
+++ b/solution.py
@@ -136,13 +136,13 @@
         bias[first : first + BLOCK, :] = jnp.where(allowed, 0.0, masked_value)
 
 
-def qkv_loads(g, chosen, own, oth, upper_width, upper_keys, weight, sems):
+def qkv_loads(g, side, own, oth, weight, sems):
     w_here = pl.ds(pl.multiple_of(g * HALF, 64), HALF)
     w_there = pl.ds(pl.multiple_of((1 - g) * HALF, 64), HALF)
     windows = (
-        (pl.multiple_of(g * 512, 128), QW, 0),
-        (pl.multiple_of(D + g * 128, 128), KW, QW),
-        (pl.multiple_of(D + KV + g * 128, 128), KW, QW + KW),
+        (pl.multiple_of(side * 512, 128), QW, 0),
+        (pl.multiple_of(D + side * 128, 128), KW, QW),
+        (pl.multiple_of(D + KV + side * 128, 128), KW, QW + KW),
     )
     loads = []
     for index, (at, width, to) in enumerate(windows):
@@ -154,12 +154,15 @@
                     sems.at[2 * index + part],
                 )
             )
-    if upper_width is None:
-        return loads
+    return loads
+
+
+def upper_loads(g, chosen, upper_width, upper_keys, weight, base, sems):
+    loads = []
     loads.append(
         copied(
             upper_width.at[0, chosen, :, pl.ds(pl.multiple_of(g * 512, 128), QW)],
-            weight.at[pl.ds(D, R), pl.ds(0, QW)],
+            weight.at[pl.ds(base, R), pl.ds(0, QW)],
             sems.at[6],
         )
     )
@@ -167,7 +170,7 @@
         loads.append(
             copied(
                 upper_keys.at[index, chosen, :, pl.ds(pl.multiple_of(g * 128, 128), KW)],
-                weight.at[pl.ds(D + (index + 1) * R, R), pl.ds(QW + index * KW, KW)],
+                weight.at[pl.ds(base + (index + 1) * R, R), pl.ds(QW + index * KW, KW)],
                 sems.at[7 + index],
             )
         )
@@ -289,7 +292,8 @@
         copied(lower_t.at[index, chosen], maps.at[pl.ds(index * R, R)], sems.at[2 + index])
         for index in range(3)
     ]
-    w_loads = qkv_loads(g, chosen, qkv_own, qkv_oth, upper_width, upper_keys, weight, w_sems)
+    w_loads = qkv_loads(g, g, qkv_own, qkv_oth, weight, w_sems)
+    w_loads += upper_loads(g, chosen, upper_width, upper_keys, weight, D, w_sems)
     for load in loads:
         load.start()
     starts = doc_starts(segments[...])
@@ -763,7 +767,7 @@
             pltpu.SemaphoreType.DMA((12,)),
             pltpu.SemaphoreType.DMA((6,)),
         ],
-        compiler_params=pltpu.CompilerParams(vmem_limit_bytes=46 << 20),
+        compiler_params=pltpu.CompilerParams(vmem_limit_bytes=44 << 20),
         cost_estimate=pl.CostEstimate(
             flops=30 * 10**9, bytes_accessed=36 << 20, transcendentals=2 * 10**6
         ),
@@ -778,9 +782,6 @@
     do_oth,
     o_in,
     normed,
-    qkv_own,
-    qkv_oth,
-    lower_t,
     upper_width,
     upper_keys,
     query_in,
@@ -801,9 +802,6 @@
         do_oth,
         o_in,
         normed,
-        qkv_own,
-        qkv_oth,
-        lower_t,
         upper_width,
         upper_keys,
         query_in,
@@ -816,9 +814,9 @@
         pack_own_in,
         pack_oth_in,
         refs[:BLOCKS],
-        refs[BLOCKS + 4 : 2 * BLOCKS + 4],
-        *refs[BLOCKS : BLOCKS + 4],
-        *refs[2 * BLOCKS + 4 :],
+        refs[BLOCKS + 3 : 2 * BLOCKS + 3],
+        *refs[BLOCKS : BLOCKS + 3],
+        *refs[2 * BLOCKS + 3 :],
     )
 
 
@@ -829,9 +827,6 @@
     do_oth,
     o_in,
     normed,
-    qkv_own,
-    qkv_oth,
-    lower_t,
     upper_width,
     upper_keys,
     query_in,
@@ -846,7 +841,6 @@
     chances_in,
     chances,
     dy_out,
-    dz_out,
     part_out,
     exchange_out,
     query,
@@ -858,10 +852,7 @@
     sine,
     pack_own,
     pack_oth,
-    inner_low,
     exchange,
-    outgoing,
-    maps,
     grad_o,
     mixed_t,
     n_rows,
@@ -888,8 +879,7 @@
     rows = length // 2
     here = pl.ds(pl.multiple_of(g * rows, 128), rows)
     there = pl.ds(pl.multiple_of((1 - g) * rows, 128), rows)
-    weight[D:, :] = jnp.zeros((128, SPAN), bf16)
-    maps[...] = jnp.zeros_like(maps)
+    weight[...] = jnp.zeros_like(weight)
     early = [
         copied(k_in, key_t, sems.at[0]),
         copied(v_in, value_t, sems.at[1]),
@@ -908,10 +898,7 @@
         copied(zt_in, zt, sems.at[10]),
         copied(pack_own_in, pack_own, sems.at[11]),
         copied(pack_oth_in, pack_oth, sems.at[12]),
-    ] + [
-        copied(lower_t.at[index, chosen], maps.at[pl.ds(index * R, R)], sems.at[13 + index])
-        for index in range(3)
-    ] + qkv_loads(g, chosen, qkv_own, qkv_oth, upper_width, upper_keys, weight, b_sems)
+    ] + upper_loads(g, chosen, upper_width, upper_keys, weight, 0, b_sems)
     kept = [
         copied(chances_in[block], chances[block], keep_sem.at[block]) for block in range(BLOCKS)
     ]
@@ -988,18 +975,15 @@
         for at in range(0, count, 128):
             side = pl.ds(pl.multiple_of(base + at + (1 - g) * HD, HD), 128)
             dy[:, to + at : to + at + 128] = dy_t[side, :].T
-    store = copied(dy.at[here], dy_out, out_sem.at[0])
-    store.start()
-    made = nt(dy[there, :], weight[...])
-    theirs = made[:, D:]
-    outgoing[...] = (made[:, :D] + nn(theirs.astype(bf16), maps[...])).astype(bf16)
-    part_store = copied(outgoing, part_out, out_sem.at[3])
-    part_store.start()
-    mine = nt(dy[here, :], weight[D:, :])
-    inner_low[...] = mine.astype(bf16)
-    inner_store = copied(inner_low, dz_out, out_sem.at[1])
-    inner_store.start()
-    gb = nn(zt[...], dy[...])
+    inner = nt(dy[:, :SPAN], weight[...])
+    dy[:, SPAN:] = inner.astype(bf16)
+    dy_stores = [
+        copied(dy.at[place], target, out_sem.at[index])
+        for place, target, index in ((there, part_out, 0), (here, dy_out, 1))
+    ]
+    for copy in dy_stores:
+        copy.start()
+    gb = nn(zt[...], dy[:, :SPAN])
     gb_q[...] = jnp.zeros_like(gb_q)
     gb_kv[...] = jnp.zeros_like(gb_kv)
     gb_q[:, pl.ds(pl.multiple_of(g * 512, 128), QW)] = gb[:R, :QW]
@@ -1007,9 +991,7 @@
         gb_kv[index, :, pl.ds(pl.multiple_of(g * 128, 128), KW)] = gb[
             (index + 1) * R : (index + 2) * R, QW + index * KW : QW + (index + 1) * KW
         ]
-    ga = nn(theirs.T[: 3 * R, :].astype(bf16), n_rows[there, :]) + nn(
-        mine.T[: 3 * R, :].astype(bf16), n_rows[here, :]
-    )
+    ga = nn(inner.T[: 3 * R, :].astype(bf16), n_rows[...])
     pack[...] = jnp.zeros_like(pack)
     packed(
         [ga[:R], ga[R : 2 * R], ga[2 * R :], gb_q[...], gb_kv[0], gb_kv[1]],
@@ -1024,7 +1006,7 @@
     ).astype(bf16)
     last = copied(exchange, exchange_out, out_sem.at[2])
     last.start()
-    for copy in (store, inner_store, part_store, last):
+    for copy in (*dy_stores, last):
         copy.wait()
 
 
@@ -1037,13 +1019,12 @@
     return pl.pallas_call(
         functools.partial(attend_back_kernel, reps),
         out_shape=[
-            shape((rows, SPAN), bf16),
-            shape((rows, 128), bf16),
-            shape((rows, D), bf16),
+            shape((rows, AUG), bf16),
+            shape((rows, AUG), bf16),
             shape((reps * R, half + width), bf16),
         ],
-        in_specs=[SMEM, HBM, ANY] + [HBM] * 15 + [ANY] + [HBM] * BLOCKS,
-        out_specs=[HBM] * 4,
+        in_specs=[SMEM, HBM, ANY] + [HBM] * 12 + [ANY] + [HBM] * BLOCKS,
+        out_specs=[HBM] * 3,
         scratch_shapes=[
             pltpu.VMEM((HEADS, (block + 1) * BLOCK, BLOCK), bf16) for block in range(BLOCKS)
         ]
@@ -1057,21 +1038,18 @@
             pltpu.VMEM((HD // 2, length), f32),
             pltpu.VMEM((reps * R, half), bf16),
             pltpu.VMEM((reps * R, half), bf16),
-            pltpu.VMEM((rows, 128), bf16),
             pltpu.VMEM((reps * R, half + width), bf16),
-            pltpu.VMEM((rows, D), bf16),
-            pltpu.VMEM((128, D), bf16),
             pltpu.VMEM((QW, length), bf16),
             pltpu.VMEM(((HEADS + 2) * HD, length), bf16),
             pltpu.VMEM((length, D), bf16),
-            pltpu.VMEM((AUG, SPAN), bf16),
+            pltpu.VMEM((128, SPAN), bf16),
             pltpu.VMEM((KEYS, length, HD), bf16),
             pltpu.VMEM((R, length), f32),
             pltpu.VMEM((HEADS, HD, length), f32),
             pltpu.VMEM((KEYS, HD, length), f32),
             pltpu.VMEM((KEYS, HD, length), f32),
             pltpu.VMEM(((HEADS + 2 * KEYS + 6) * HD, length), bf16),
-            pltpu.VMEM((length, SPAN), bf16),
+            pltpu.VMEM((length, AUG), bf16),
             pltpu.VMEM((GROUP, length, BLOCK), bf16),
             pltpu.VMEM((R, D), f32),
             pltpu.VMEM((2, R, KV), f32),
@@ -1092,7 +1070,6 @@
 def finish_kernel(
     adapter,
     dy_in,
-    dz_in,
     qkv_own,
     qkv_oth,
     lower_t,
@@ -1103,11 +1080,11 @@
     middle_in,
     out,
     dy,
-    dz,
+    part,
     tok,
-    part,
     grad_middle,
     weight,
+    weight_oth,
     maps,
     result,
     sems,
@@ -1117,9 +1094,10 @@
     g = lax.axis_index("grp")
     chosen = adapter[0]
     maps[...] = jnp.zeros_like(maps)
-    loads = qkv_loads(g, chosen, qkv_own, qkv_oth, None, None, weight, w_sems)
+    loads = qkv_loads(g, g, qkv_own, qkv_oth, weight, w_sems.at[0])
+    loads += qkv_loads(g, 1 - g, qkv_own, qkv_oth, weight_oth, w_sems.at[1])
     for index, (source, target) in enumerate(
-        ((dy_in, dy), (dz_in, dz), (tok_in, tok), (middle_in, grad_middle), (part_in, part))
+        ((dy_in, dy), (part_in, part), (tok_in, tok), (middle_in, grad_middle))
     ):
         loads.append(copied(source, target, sems.at[index]))
     for index in range(3):
@@ -1135,7 +1113,12 @@
     def half(index, carry):
         count = tok.shape[0] // 2
         span = pl.ds(pl.multiple_of(index * count, 128), count)
-        grad = nt(dy[span, :], weight[...]) + nn(dz[span, :], maps[...]) + part[span, :].astype(f32)
+        inner = dy[span, SPAN:].astype(f32) + part[span, SPAN:].astype(f32)
+        grad = (
+            nt(dy[span, :SPAN], weight[...])
+            + nt(part[span, :SPAN], weight_oth[...])
+            + nn(inner.astype(bf16), maps[...])
+        )
         result[span, :] = (
             grad_middle[span, :] + normed_back(tok[span, :].astype(f32), gain, grad)
         ).astype(bf16)
@@ -1152,22 +1135,22 @@
     return pl.pallas_call(
         finish_kernel,
         out_shape=jax.ShapeDtypeStruct((rows, D), bf16),
-        in_specs=[SMEM] + [HBM] * 6 + [VMEM] * 2 + [ANY, HBM],
+        in_specs=[SMEM] + [HBM] * 5 + [VMEM] * 2 + [ANY, HBM],
         out_specs=HBM,
         scratch_shapes=[
-            pltpu.VMEM((rows, SPAN), bf16),
-            pltpu.VMEM((rows, 128), bf16),
-            pltpu.VMEM((rows, D), bf16),
+            pltpu.VMEM((rows, AUG), bf16),
+            pltpu.VMEM((rows, AUG), bf16),
             pltpu.VMEM((rows, D), bf16),
             pltpu.VMEM((rows, D), f32),
+            pltpu.VMEM((D, SPAN), bf16),
             pltpu.VMEM((D, SPAN), bf16),
             pltpu.VMEM((128, D), bf16),
             pltpu.VMEM((rows, D), bf16),
             pltpu.SemaphoreType.DMA((8,)),
-            pltpu.SemaphoreType.DMA((6,)),
+            pltpu.SemaphoreType.DMA((2, 6)),
             pltpu.SemaphoreType.DMA((1,)),
         ],
-        compiler_params=pltpu.CompilerParams(vmem_limit_bytes=VMEM_BYTES),
+        compiler_params=pltpu.CompilerParams(vmem_limit_bytes=50 << 20),
         cost_estimate=pl.CostEstimate(
             flops=4 * 10**9, bytes_accessed=10 << 20, transcendentals=0
         ),
@@ -1331,16 +1314,13 @@
     )
     do_oth = swap(do_send)
     pack_oth = swap(pack_send)
-    dy, dz, part_send, exchange = attend_back(
+    dy, dy_send, exchange = attend_back(
         reps,
         adapter_ids,
         do_own,
         do_oth,
         mixed_t,
         normed,
-        frozen_qkv,
-        qkv_oth,
-        lower_t,
         upper_width,
         upper_keys,
         query,
@@ -1358,13 +1338,12 @@
     input_grad = finish(
         adapter_ids,
         dy,
-        dz,
         frozen_qkv,
         qkv_oth,
         lower_t,
         tok_own,
         *gains,
-        swap(part_send),
+        swap(dy_send),
         grad_middle,
     )
     received, input_grad = lax.optimization_barrier((received, input_grad))

time: 127 us -> 123 us (0.969)
  waiting for transfers between devices: 14.3 us -> 11.8 us
    all_to_all x1, waiting for transfers between devices: 4.7 us -> 2.13 us  [per_device(): received = lax.all_to_all(exchange, 'rep', 0, 0, tiled=True)]
    pallas_call x1, Pallas kernels: 24.3 us -> 22.1 us  [attend_back(): pl.pallas_call(functools.partial(attend_back_kernel, reps), out_shape=[sh...]
    unnamed x26 -> x22, local copies, waits for them, and re-layouts: 3.5 us -> 2.63 us
  transfers between devices with their start and end apart: 12 -> 12, of which waited for: 6 -> 6; matrix products, arithmetic and copies ran while one was open for 0% -> 0% of each run, Pallas kernels for 24% -> 25%
where the time goes in v2:
time: 123 us
  Pallas kernels  95.1 us (77%)
  waiting for transfers between devices  11.8 us (10%)
  starting transfers between devices  11.2 us (9%)
  local copies, waits for them, and re-layouts  3.18 us (3%)
  between operations  1.49 us (1%)
    pallas_call x1, Pallas kernels, feed(): pl.pallas_call(functools.partial(feed_kernel, reps), out_shape=[shape((ro...  40.2 us
    pallas_call x1, Pallas kernels, attend_back(): pl.pallas_call(functools.partial(attend_back_kernel, reps), out_shape=[sh...  22.1 us
    pallas_call x1, Pallas kernels, attend(): pl.pallas_call(attend_kernel, out_shape=[shape((rows, QW), bf16), shape((...  21.7 us
    ppermute x11, waiting for transfers between devices, per_device(): swap = lambda value: lax.ppermute(value, 'grp', SWAP)  9.67 us
    pallas_call x1, Pallas kernels, finish(): pl.pallas_call(finish_kernel, out_shape=jax.ShapeDtypeStruct((rows, D), b...  9.44 us
    all_to_all x1, starting transfers between devices, per_device(): received = lax.all_to_all(exchange, 'rep', 0, 0, tiled=True)  8.21 us
    ppermute x11, starting transfers between devices, per_device(): swap = lambda value: lax.ppermute(value, 'grp', SWAP)  2.94 us
    unnamed x22, local copies, waits for them, and re-layouts  2.63 us
  transfers between devices with their start and end apart: 12, of which 6 were waited for; matrix products, arithmetic and copies ran while one was open for 0% of the time, Pallas kernels for 25%

profile of v2, /device:TPU:0, one launch (start us, length us, event | category | flops | bytes accessed | tf_op | source)
XLA Modules:
  0.0 122.7 jit_solution(14200646850447049324)
XLA Ops:
  0.6 0.0 copy-start
  0.7 0.0 copy-start.9
  0.7 0.0 copy-start.2
  0.7 0.0 copy-start.6
  0.7 0.0 copy-start.7
  0.7 0.0 copy-start.8
  0.7 0.5 collective-permute-start.1
  1.2 0.1 collective-permute-start
  1.3 0.4 collective-permute-start.2
  2.4 0.0 copy-done
  2.4 0.4 copy.21
  2.8 0.2 pad.4.a_down
  3.0 2.4 %collective-permute-done.2.gains_oth = bf16[2,576]{1,0:T(2,128)(2,1)S(1)} collective-permute-done((bf16[2,576]{1,0:T(2,128)(2,1)}, bf16[2,576]{1,0:T(2,128)(2,1)S(1)}, u32[]{:S(2)}, u32[]{:S(2)}) %collective-permute-start.2) | collective-permute-done | bytes 2336 | tf_op jit(solution)/shard_map/ppermute | solution.py:1262
  5.4 1.8 %collective-permute-done.tok_oth = bf16[512,1152]{1,0:T(8,128)(2,1)} collective-permute-done((bf16[512,1152]{1,0:T(8,128)(2,1)}, bf16[512,1152]{1,0:T(8,128)(2,1)}, u32[]{:S(2)}, u32[]{:S(2)}) %collective-permute-start) | collective-permute-done | bytes 1179680 | tf_op jit(solution)/shard_map/ppermute | solution.py:1262
  7.2 0.0 collective-permute-done.1.qkv_oth
  7.2 0.4 collective-permute-start.5
  7.6 0.1 collective-permute-start.6
  7.7 0.0 copy-done.2
  7.7 0.4 collective-permute-start.4
  8.1 0.0 copy-done.9
  8.1 0.0 copy-done.6
  8.1 0.0 copy-start.3
  8.1 0.0 copy-start.4
  8.1 21.7 %attend.1 = (bf16[512,640]{1,0:T(8,128)(2,1)S(1)}, bf16[512,640]{1,0:T(8,128)(2,1)S(1)}, bf16[640,1024]{1,0:T(8,128)(2,1)}, bf16[256,1024]{1,0:T(8,128)(2,1)S(1)...) custom-call(s32[1]{0:T(128)} %copy.22.adapter, ...), custom_call_target="tpu_custom_call" | custom-call | flops 16000000000 | bytes 16777216 | tf_op jit(solution)/shard_map/attend/pallas_call | solution.py:416
  29.8 0.2 collective-permute-start.3
  30.0 2.0 %collective-permute-done.3.o_oth_in = bf16[512,640]{1,0:T(8,128)(2,1)S(1)} collective-permute-done((bf16[512,640]{1,0:T(8,128)(2,1)S(1)}, bf16[512,640]{1,0:T(8,128)(2,1)S(1)}, u32[]{:S(2)}, u32[]{:S(2)}) %collective-permute-start.3) | collective-permute-done | bytes 655392 | tf_op jit(solution)/shard_map/ppermute | solution.py:1262
  32.0 0.0 collective-permute-done.4.wo_oth
  32.0 0.0 collective-permute-done.6.wd_oth
  32.0 0.0 collective-permute-done.5.wgu_oth
  32.0 40.2 %feed.1 = (bf16[512,1152]{1,0:T(8,128)(2,1)}, f32[512,1152]{1,0:T(8,128)}, bf16[640,512]{1,0:T(8,128)(2,1)S(1)}, bf16[640,512]{1,0:T(8,128)(2,1)S(1)}, bf16[256,...) custom-call(s32[1]{0:T(128)} %copy.22.adapter, bf16[512,640]{1,0:T(8,128)(2,1)S(1)} %get-tuple-element.50.o_own_in, ...), custom_call_target="tpu_custom_call" | custom-call | flops 30000001024 | bytes 37748736 | tf_op jit(solution)/shard_map/feed/pallas_call | solution.py:729
  72.3 0.2 collective-permute-start.7
  72.5 0.4 collective-permute-start.8
  72.8 2.0 %collective-permute-done.8.pack_oth_in = bf16[256,512]{1,0:T(8,128)(2,1)S(1)} collective-permute-done((bf16[256,512]{1,0:T(8,128)(2,1)S(1)}, bf16[256,512]{1,0:T(8,128)(2,1)S(1)}, u32[]{:S(2)}, u32[]{:S(2)}) %collective-permute-start.8) | collective-permute-done | bytes 262176 | tf_op jit(solution)/shard_map/ppermute | solution.py:1262
  74.8 0.0 collective-permute-done.7.do_oth
  74.8 22.1 %attend_back.1 = (bf16[512,1280]{1,0:T(8,128)(2,1)}, bf16[512,1280]{1,0:T(8,128)(2,1)}, bf16[256,896]{1,0:T(8,128)(2,1)}) custom-call(s32[1]{0:T(128)} %copy.22.adapter, bf16[640,512]{1,0:T(8,128)(2,1)S(1)} %get-tuple-element.57.do_own, bf16[640,512]{1,0:T(8,128)(2,1)S(1)} %collective-permute-done.7.do_oth, bf16[704,1024]{1,0:T(8,128)(2,1)} %get-tuple-element.59.o_in, ...), custom_call_target="tpu_custom_call" | custom-call | flops 24000000000 | bytes 20971520 | tf_op jit(solution)/shard_map/attend_back/pallas_call | solution.py:1019
  96.9 0.2 collective-permute-start.9
  97.1 8.2 %all-to-all-start = ((bf16[16,16,896]{2,1,0:T(8,128)(2,1)}), bf16[16,16,896]{2,1,0:T(8,128)(2,1)S(1)}, u32[]{:S(2)}, u32[]{:S(2)}) async-start(bf16[16,16,896]{2,1,0:T(8,128)(2,1)} %bitcast.6), calls=%async_computation | async-start | bytes 917504 | tf_op jit(solution)/shard_map/all_to_all | solution.py:1337
  105.4 0.0 collective-permute-done.9.part_in
  105.4 0.0 copy-start.5
  105.4 1.3 %copy-done.5 = bf16[1,512,1152]{2,1,0:T(8,128)(2,1)S(1)} copy-done((bf16[1,512,1152]{2,1,0:T(8,128)(2,1)S(1)}, bf16[1,512,1152]{2,1,0:T(8,128)(2,1)}, u32[]{:S(2)}) %copy-start.5) | copy-done | bytes 1179672
  106.6 1.3 %copy-done.10 = bf16[512,1280]{1,0:T(8,128)(2,1)S(1)} copy-done((bf16[512,1280]{1,0:T(8,128)(2,1)S(1)}, bf16[512,1280]{1,0:T(8,128)(2,1)}, u32[]{:S(2)}) %copy-start.10) | copy-done | bytes 1310744
  108.0 9.4 %finish.1 = bf16[512,1152]{1,0:T(8,128)(2,1)} custom-call(s32[1]{0:T(128)} %copy.22.adapter, bf16[512,1280]{1,0:T(8,128)(2,1)S(1)} %copy-done.10, bf16[576,1920]{1,0:T(8,128)(2,1)} %qkv_own.3, bf16[576,1920]{1,0:T(8,128)(2,1)} %collective-permute-done.1.qkv_oth, bf16[6,8,16,1152]{3,2,1,0:T(8,128)(2,1)} %bitcast.23, bf16[512,1152]{1,0:T(8,128)(2,1)S(1)} %bitcast.19, ...), custom_call_target="tpu_custom_call" | custom-call | flops 4000000000 | bytes 10485760 | tf_op jit(solution)/shard_map/finish/pallas_call | solution.py:1135
  117.4 2.1 %all-to-all-done = bf16[16,16,896]{2,1,0:T(8,128)(2,1)S(1)} async-done(((bf16[16,16,896]{2,1,0:T(8,128)(2,1)}), bf16[16,16,896]{2,1,0:T(8,128)(2,1)S(1)}, u32[]{:S(2)}, u32[]{:S(2)}) %all-to-all-start) | async-done | bytes 458784 | tf_op jit(solution)/shard_map/all_to_all | solution.py:1337
  119.5 0.6 collect.1
  120.2 0.1 collective-permute-start.10
  120.2 1.5 %collective-permute-done.10.other = f32[4,16,896]{2,1,0:T(8,128)S(1)} collective-permute-done((f32[4,16,896]{2,1,0:T(8,128)S(1)}, f32[4,16,896]{2,1,0:T(8,128)S(1)}, u32[]{:S(2)}, u32[]{:S(2)}) %collective-permute-start.10) | collective-permute-done | bytes 229408 | tf_op jit(solution)/shard_map/ppermute | solution.py:1262
  121.7 1.0 deliver.1
  122.7 0.0 copy-done.1
  (7 shorter events, 0.0 us)
Async XLA Ops:
  0.6 1.8 %copy-start = (bf16[8,3072,16]{1,2,0:T(8,128)(2,1)S(1)}, bf16[8,3072,16]{1,2,0:T(8,128)(2,1)}, u32[]{:S(2)}) copy-start(bf16[8,3072,16]{1,2,0:T(8,128)(2,1)} %param.24) | copy-start | bytes 2359300
  0.7 7.4 %copy-start.9 = (bf16[2,576]{1,0:T(2,128)(2,1)S(1)}, bf16[2,576]{1,0:T(2,128)(2,1)}, u32[]{:S(2)}) copy-start(bf16[2,576]{1,0:T(2,128)(2,1)} %gains_own.5) | copy-start | bytes 6916
  0.7 7.1 %copy-start.2 = (bf16[576,1152]{1,0:T(8,128)(2,1)S(1)}, bf16[576,1152]{1,0:T(8,128)(2,1)}, u32[]{:S(2)}) copy-start(bf16[576,1152]{1,0:T(8,128)(2,1)} %wo_own.1) | copy-start | bytes 3981316
  0.7 7.4 %copy-start.6 = (bf16[3,8,16,1152]{3,2,1,0:T(8,128)(2,1)S(1)}, bf16[3,8,16,1152]{3,2,1,0:T(8,128)(2,1)}, u32[]{:S(2)}) copy-start(bf16[3,8,16,1152]{3,2,1,0:T(8,128)(2,1)} %upper_width.5) | copy-start | bytes 2654212
  0.7 7.4 %copy-start.7 = (bf16[2,8,16,384]{3,2,1,0:T(8,128)(2,1)S(1)}, bf16[2,8,16,384]{3,2,1,0:T(8,128)(2,1)}, u32[]{:S(2)}) copy-start(bf16[2,8,16,384]{3,2,1,0:T(8,128)(2,1)} %upper_keys.3) | copy-start | bytes 589828
  0.7 7.4 %copy-start.8 = (s32[1,1024]{1,0:T(1,128)S(1)}, s32[1,1024]{1,0:T(1,128)}, u32[]{:S(2)}) copy-start(s32[1,1024]{1,0:T(1,128)} %segments.1) | copy-start | bytes 12292
  0.7 6.5 %collective-permute-start.1 = (bf16[576,1920]{1,0:T(8,128)(2,1)}, bf16[576,1920]{1,0:T(8,128)(2,1)}, u32[]{:S(2)}, u32[]{:S(2)}) collective-permute-start(bf16[576,1920]{1,0:T(8,128)(2,1)} %qkv_own.3), channel_id=1, source_target_pairs={{0,16},{16,0},{1,17},{17,1},{2,18},{18,2},{3,19},{19,3},{4,20},{20... | collective-permute-start | bytes 6635528 | tf_op jit(solution)/shard_map/ppermute | solution.py:1262
  1.2 6.0 %collective-permute-start = (bf16[512,1152]{1,0:T(8,128)(2,1)}, bf16[512,1152]{1,0:T(8,128)(2,1)}, u32[]{:S(2)}, u32[]{:S(2)}) collective-permute-start(bf16[512,1152]{1,0:T(8,128)(2,1)} %bitcast.16), channel_id=1, source_target_pairs={{0,16},{16,0},{1,17},{17,1},{2,18},{18,2},{3,19},{19,3},{4,20},{20... | collective-permute-start | bytes 3538952 | tf_op jit(solution)/shard_map/ppermute | solution.py:1262
  1.3 4.1 %collective-permute-start.2 = (bf16[2,576]{1,0:T(2,128)(2,1)}, bf16[2,576]{1,0:T(2,128)(2,1)S(1)}, u32[]{:S(2)}, u32[]{:S(2)}) collective-permute-start(bf16[2,576]{1,0:T(2,128)(2,1)} %gains_own.5), channel_id=1, source_target_pairs={{0,16},{16,0},{1,17},{17,1},{2,18},{18,2},{3,19},{19,3},{4,20},{20... | collective-permute-start | bytes 6920 | tf_op jit(solution)/shard_map/ppermute | solution.py:1262
  7.2 24.8 %collective-permute-start.5 = (bf16[576,6144]{1,0:T(8,128)(2,1)}, bf16[576,6144]{1,0:T(8,128)(2,1)}, u32[]{:S(2)}, u32[]{:S(2)}) collective-permute-start(bf16[576,6144]{1,0:T(8,128)(2,1)} %wgu_own.1), channel_id=1, source_target_pairs={{0,16},{16,0},{1,17},{17,1},{2,18},{18,2},{3,19},{19,3},{4,20},{20... | collective-permute-start | bytes 21233672 | tf_op jit(solution)/shard_map/ppermute | solution.py:1262
  7.6 24.4 %collective-permute-start.6 = (bf16[1536,1152]{1,0:T(8,128)(2,1)}, bf16[1536,1152]{1,0:T(8,128)(2,1)}, u32[]{:S(2)}, u32[]{:S(2)}) collective-permute-start(bf16[1536,1152]{1,0:T(8,128)(2,1)} %wd_own.1), channel_id=1, source_target_pairs={{0,16},{16,0},{1,17},{17,1},{2,18},{18,2},{3,19},{19,3},{4,20},{20... | collective-permute-start | bytes 10616840 | tf_op jit(solution)/shard_map/ppermute | solution.py:1262
  7.7 24.3 %collective-permute-start.4 = (bf16[576,1152]{1,0:T(8,128)(2,1)S(1)}, bf16[576,1152]{1,0:T(8,128)(2,1)S(1)}, u32[]{:S(2)}, u32[]{:S(2)}) collective-permute-start(bf16[576,1152]{1,0:T(8,128)(2,1)S(1)} %copy-done.2), channel_id=1, source_target_pairs={{0,16},{16,0},{1,17},{17,1},{2,18},{18,2},{3,19},{19,3},{4,20},{20... | collective-permute-start | bytes 3981320 | tf_op jit(solution)/shard_map/ppermute | solution.py:1262
  8.1 23.9 %copy-start.3 = (bf16[1,512,1152]{2,1,0:T(8,128)(2,1)S(1)}, bf16[1,512,1152]{2,1,0:T(8,128)(2,1)}, u32[]{:S(2)}) copy-start(bf16[1,512,1152]{2,1,0:T(8,128)(2,1)} %param.15) | copy-start | bytes 3538948
  8.1 23.9 %copy-start.4 = (bf16[1,512,1152]{2,1,0:T(8,128)(2,1)S(1)}, bf16[1,512,1152]{2,1,0:T(8,128)(2,1)}, u32[]{:S(2)}) copy-start(bf16[1,512,1152]{2,1,0:T(8,128)(2,1)} %param.14) | copy-start | bytes 3538948
  29.8 2.2 %collective-permute-start.3 = (bf16[512,640]{1,0:T(8,128)(2,1)S(1)}, bf16[512,640]{1,0:T(8,128)(2,1)S(1)}, u32[]{:S(2)}, u32[]{:S(2)}) collective-permute-start(bf16[512,640]{1,0:T(8,128)(2,1)S(1)} %get-tuple-element.51), channel_id=1, source_target_pairs={{0,16},{16,0},{1,17},{17,1},{2,18},{18,2},{3,19},{19,3},{4,20},{20... | collective-permute-start | bytes 1966088 | tf_op jit(solution)/shard_map/ppermute | solution.py:1262
  72.3 2.5 %collective-permute-start.7 = (bf16[640,512]{1,0:T(8,128)(2,1)S(1)}, bf16[640,512]{1,0:T(8,128)(2,1)S(1)}, u32[]{:S(2)}, u32[]{:S(2)}) collective-permute-start(bf16[640,512]{1,0:T(8,128)(2,1)S(1)} %get-tuple-element.58), channel_id=1, source_target_pairs={{0,16},{16,0},{1,17},{17,1},{2,18},{18,2},{3,19},{19,3},{4,20},{20... | collective-permute-start | bytes 1966088 | tf_op jit(solution)/shard_map/ppermute | solution.py:1262
  72.5 2.3 %collective-permute-start.8 = (bf16[256,512]{1,0:T(8,128)(2,1)S(1)}, bf16[256,512]{1,0:T(8,128)(2,1)S(1)}, u32[]{:S(2)}, u32[]{:S(2)}) collective-permute-start(bf16[256,512]{1,0:T(8,128)(2,1)S(1)} %get-tuple-element.69), channel_id=1, source_target_pairs={{0,16},{16,0},{1,17},{17,1},{2,18},{18,2},{3,19},{19,3},{4,20},{20... | collective-permute-start | bytes 786440 | tf_op jit(solution)/shard_map/ppermute | solution.py:1262
  96.9 8.4 %collective-permute-start.9 = (bf16[512,1280]{1,0:T(8,128)(2,1)}, bf16[512,1280]{1,0:T(8,128)(2,1)S(1)}, u32[]{:S(2)}, u32[]{:S(2)}) collective-permute-start(bf16[512,1280]{1,0:T(8,128)(2,1)} %get-tuple-element.76), channel_id=1, source_target_pairs={{0,16},{16,0},{1,17},{17,1},{2,18},{18,2},{3,19},{19,3},{4,20},{20... | collective-permute-start | bytes 3932168 | tf_op jit(solution)/shard_map/ppermute | solution.py:1262
  97.1 22.4 %all-to-all-start = ((bf16[16,16,896]{2,1,0:T(8,128)(2,1)}), bf16[16,16,896]{2,1,0:T(8,128)(2,1)S(1)}, u32[]{:S(2)}, u32[]{:S(2)}) async-start(bf16[16,16,896]{2,1,0:T(8,128)(2,1)} %bitcast.6), calls=%async_computation | async-start | bytes 917504 | tf_op jit(solution)/shard_map/all_to_all | solution.py:1337
  105.4 1.3 %copy-start.5 = (bf16[1,512,1152]{2,1,0:T(8,128)(2,1)S(1)}, bf16[1,512,1152]{2,1,0:T(8,128)(2,1)}, u32[]{:S(2)}) copy-start(bf16[1,512,1152]{2,1,0:T(8,128)(2,1)} %param.14) | copy-start | bytes 3538948
  106.6 1.3 %copy-start.10 = (bf16[512,1280]{1,0:T(8,128)(2,1)S(1)}, bf16[512,1280]{1,0:T(8,128)(2,1)}, u32[]{:S(2)}) copy-start(bf16[512,1280]{1,0:T(8,128)(2,1)} %get-tuple-element.75.dy_in) | copy-start | bytes 3932164
  108.0 14.7 %copy-start.1 = (bf16[8,3072,16]{1,2,0:T(8,128)(2,1)S(1)}, bf16[8,3072,16]{1,2,0:T(8,128)(2,1)}, u32[]{:S(2)}) copy-start(bf16[8,3072,16]{1,2,0:T(8,128)(2,1)} %param.24) | copy-start | bytes 2359300
  120.2 1.6 %collective-permute-start.10 = (f32[4,16,896]{2,1,0:T(8,128)S(1)}, f32[4,16,896]{2,1,0:T(8,128)S(1)}, u32[]{:S(2)}, u32[]{:S(2)}) collective-permute-start(f32[4,16,896]{2,1,0:T(8,128)S(1)} %get-tuple-element.81), channel_id=1, source_target_pairs={{0,16},{16,0},{1,17},{17,1},{2,18},{18,2},{3,19},{19,3},{4,20},{20... | collective-permute-start | bytes 688136 | tf_op jit(solution)/shard_map/ppermute | solution.py:1262

commit v3 on v2

--- a/solution.py
+++ b/solution.py
@@ -391,7 +391,14 @@
                 top = later
             return top
 
-        lax.fori_loop(0, KEYS, group, score(0, 0))
+        if block < BLOCKS - 1:
+            lax.fori_loop(0, KEYS, group, score(0, 0))
+        else:
+            top = score(0, 0)
+            for h in range(HEADS):
+                later = score(h + 1, (h + 1) % GROUP) if h + 1 < HEADS else None
+                blend(h, h % GROUP, top)
+                top = later
         stores.append(copied(kept, chances_out[block], keep_sem.at[block]))
         stores[-1].start()
         for pair in range(QW // 128):
@@ -659,14 +666,28 @@
             start(step + 1, 1 - slot)
 
         wait(step, slot)
-        gate = nn(normed[...], wg[slot])
-        up = nn(normed[...], wu[slot])
-        grad_active = nt(cot_aug[...], wd[slot])
-        sigmoid = 1.0 / (1.0 + jnp.exp(-gate))
-        silu = gate * sigmoid
-        active = (silu * up).astype(bf16)
-        grad_gate = (grad_active * up * (sigmoid * (1.0 + gate * (1.0 - sigmoid)))).astype(bf16)
-        grad_up = (grad_active * silu).astype(bf16)
+        parts = []
+        for at in range(0, TILE, 256):
+            cols = slice(at, at + 256)
+            parts.append(
+                (
+                    nn(normed[...], wg[slot, :, cols]),
+                    nn(normed[...], wu[slot, :, cols]),
+                    nt(cot_aug[...], wd[slot, cols, :]),
+                )
+            )
+        acts, gates, ups = [], [], []
+        for gate, up, grad_active in parts:
+            sigmoid = 1.0 / (1.0 + jnp.exp(-gate))
+            silu = gate * sigmoid
+            acts.append((silu * up).astype(bf16))
+            gates.append(
+                (grad_active * up * (sigmoid * (1.0 + gate * (1.0 - sigmoid)))).astype(bf16)
+            )
+            ups.append((grad_active * silu).astype(bf16))
+        active = jnp.concatenate(acts, axis=1)
+        grad_gate = jnp.concatenate(gates, axis=1)
+        grad_up = jnp.concatenate(ups, axis=1)
         total[...] += nn(active, wd[slot])
         back[...] += nt(grad_gate, wg[slot]) + nt(grad_up, wu[slot])
         shares = (

time: 123 us -> 122 us (level)
  no operation moved by 1% of the time
where the time goes in v3:
time: 122 us
  Pallas kernels  94.1 us (77%)
  waiting for transfers between devices  11.8 us (10%)
  starting transfers between devices  11.2 us (9%)
  local copies, waits for them, and re-layouts  3.18 us (3%)
  between operations  1.49 us (1%)
    pallas_call x1, Pallas kernels, feed(): pl.pallas_call(functools.partial(feed_kernel, reps), out_shape=[shape((ro...  40 us
    pallas_call x1, Pallas kernels, attend_back(): pl.pallas_call(functools.partial(attend_back_kernel, reps), out_shape=[sh...  21.9 us
    pallas_call x1, Pallas kernels, attend(): pl.pallas_call(attend_kernel, out_shape=[shape((rows, QW), bf16), shape((...  21.2 us
    ppermute x11, waiting for transfers between devices, per_device(): swap = lambda value: lax.ppermute(value, 'grp', SWAP)  9.66 us
    pallas_call x1, Pallas kernels, finish(): pl.pallas_call(finish_kernel, out_shape=jax.ShapeDtypeStruct((rows, D), b...  9.44 us
    all_to_all x1, starting transfers between devices, per_device(): received = lax.all_to_all(exchange, 'rep', 0, 0, tiled=True)  8.23 us
    ppermute x11, starting transfers between devices, per_device(): swap = lambda value: lax.ppermute(value, 'grp', SWAP)  2.95 us
    unnamed x22, local copies, waits for them, and re-layouts  2.63 us
  transfers between devices with their start and end apart: 12, of which 6 were waited for; matrix products, arithmetic and copies ran while one was open for 0% of the time, Pallas kernels for 25%

profile of v3, /device:TPU:0, one launch (start us, length us, event | category | flops | bytes accessed | tf_op | source)
XLA Modules:
  0.0 121.7 jit_solution(7636029876447332527)
XLA Ops:
  0.6 0.0 copy-start
  0.7 0.0 copy-start.9
  0.7 0.0 copy-start.2
  0.7 0.0 copy-start.6
  0.7 0.0 copy-start.7
  0.7 0.0 copy-start.8
  0.7 0.5 collective-permute-start.1
  1.2 0.1 collective-permute-start
  1.3 0.4 collective-permute-start.2
  2.4 0.0 copy-done
  2.4 0.4 copy.21
  2.8 0.2 pad.4.a_down
  3.0 2.4 %collective-permute-done.2.gains_oth = bf16[2,576]{1,0:T(2,128)(2,1)S(1)} collective-permute-done((bf16[2,576]{1,0:T(2,128)(2,1)}, bf16[2,576]{1,0:T(2,128)(2,1)S(1)}, u32[]{:S(2)}, u32[]{:S(2)}) %collective-permute-start.2) | collective-permute-done | bytes 2336 | tf_op jit(solution)/shard_map/ppermute | solution.py:1283
  5.4 1.8 %collective-permute-done.tok_oth = bf16[512,1152]{1,0:T(8,128)(2,1)} collective-permute-done((bf16[512,1152]{1,0:T(8,128)(2,1)}, bf16[512,1152]{1,0:T(8,128)(2,1)}, u32[]{:S(2)}, u32[]{:S(2)}) %collective-permute-start) | collective-permute-done | bytes 1179680 | tf_op jit(solution)/shard_map/ppermute | solution.py:1283
  7.2 0.0 collective-permute-done.1.qkv_oth
  7.2 0.4 collective-permute-start.5
  7.6 0.1 collective-permute-start.6
  7.7 0.0 copy-done.2
  7.7 0.4 collective-permute-start.4
  8.1 0.0 copy-done.9
  8.1 0.0 copy-done.6
  8.1 0.0 copy-done.7
  8.1 0.0 copy-start.3
  8.1 0.0 copy-start.4
  8.1 21.2 %attend.1 = (bf16[512,640]{1,0:T(8,128)(2,1)S(1)}, bf16[512,640]{1,0:T(8,128)(2,1)S(1)}, bf16[640,1024]{1,0:T(8,128)(2,1)}, bf16[256,1024]{1,0:T(8,128)(2,1)S(1)...) custom-call(s32[1]{0:T(128)} %copy.22.adapter, ...), custom_call_target="tpu_custom_call" | custom-call | flops 16000000000 | bytes 16777216 | tf_op jit(solution)/shard_map/attend/pallas_call | solution.py:423
  29.3 0.2 collective-permute-start.3
  29.5 2.0 %collective-permute-done.3.o_oth_in = bf16[512,640]{1,0:T(8,128)(2,1)S(1)} collective-permute-done((bf16[512,640]{1,0:T(8,128)(2,1)S(1)}, bf16[512,640]{1,0:T(8,128)(2,1)S(1)}, u32[]{:S(2)}, u32[]{:S(2)}) %collective-permute-start.3) | collective-permute-done | bytes 655392 | tf_op jit(solution)/shard_map/ppermute | solution.py:1283
  31.5 0.0 collective-permute-done.4.wo_oth
  31.5 0.0 collective-permute-done.6.wd_oth
  31.5 0.0 collective-permute-done.5.wgu_oth
  31.5 40.0 %feed.1 = (bf16[512,1152]{1,0:T(8,128)(2,1)}, f32[512,1152]{1,0:T(8,128)}, bf16[640,512]{1,0:T(8,128)(2,1)S(1)}, bf16[640,512]{1,0:T(8,128)(2,1)S(1)}, bf16[256,...) custom-call(s32[1]{0:T(128)} %copy.22.adapter, bf16[512,640]{1,0:T(8,128)(2,1)S(1)} %get-tuple-element.50.o_own_in, ...), custom_call_target="tpu_custom_call" | custom-call | flops 30000001024 | bytes 37748736 | tf_op jit(solution)/shard_map/feed/pallas_call | solution.py:750
  71.5 0.2 collective-permute-start.7
  71.7 0.4 collective-permute-start.8
  72.1 2.0 %collective-permute-done.8.pack_oth_in = bf16[256,512]{1,0:T(8,128)(2,1)S(1)} collective-permute-done((bf16[256,512]{1,0:T(8,128)(2,1)S(1)}, bf16[256,512]{1,0:T(8,128)(2,1)S(1)}, u32[]{:S(2)}, u32[]{:S(2)}) %collective-permute-start.8) | collective-permute-done | bytes 262176 | tf_op jit(solution)/shard_map/ppermute | solution.py:1283
  74.0 0.0 collective-permute-done.7.do_oth
  74.0 21.9 %attend_back.1 = (bf16[512,1280]{1,0:T(8,128)(2,1)}, bf16[512,1280]{1,0:T(8,128)(2,1)}, bf16[256,896]{1,0:T(8,128)(2,1)}) custom-call(s32[1]{0:T(128)} %copy.22.adapter, bf16[640,512]{1,0:T(8,128)(2,1)S(1)} %get-tuple-element.57.do_own, bf16[640,512]{1,0:T(8,128)(2,1)S(1)} %collective-permute-done.7.do_oth, bf16[704,1024]{1,0:T(8,128)(2,1)} %get-tuple-element.59.o_in, ...), custom_call_target="tpu_custom_call" | custom-call | flops 24000000000 | bytes 20971520 | tf_op jit(solution)/shard_map/attend_back/pallas_call | solution.py:1040
  95.9 0.2 collective-permute-start.9
  96.1 8.2 %all-to-all-start = ((bf16[16,16,896]{2,1,0:T(8,128)(2,1)}), bf16[16,16,896]{2,1,0:T(8,128)(2,1)S(1)}, u32[]{:S(2)}, u32[]{:S(2)}) async-start(bf16[16,16,896]{2,1,0:T(8,128)(2,1)} %bitcast.6), calls=%async_computation | async-start | bytes 917504 | tf_op jit(solution)/shard_map/all_to_all | solution.py:1358
  104.4 0.0 collective-permute-done.9.part_in
  104.4 0.0 copy-start.5
  104.4 1.3 %copy-done.5 = bf16[1,512,1152]{2,1,0:T(8,128)(2,1)S(1)} copy-done((bf16[1,512,1152]{2,1,0:T(8,128)(2,1)S(1)}, bf16[1,512,1152]{2,1,0:T(8,128)(2,1)}, u32[]{:S(2)}) %copy-start.5) | copy-done | bytes 1179672
  105.7 1.3 %copy-done.10 = bf16[512,1280]{1,0:T(8,128)(2,1)S(1)} copy-done((bf16[512,1280]{1,0:T(8,128)(2,1)S(1)}, bf16[512,1280]{1,0:T(8,128)(2,1)}, u32[]{:S(2)}) %copy-start.10) | copy-done | bytes 1310744
  107.0 9.4 %finish.1 = bf16[512,1152]{1,0:T(8,128)(2,1)} custom-call(s32[1]{0:T(128)} %copy.22.adapter, bf16[512,1280]{1,0:T(8,128)(2,1)S(1)} %copy-done.10, bf16[576,1920]{1,0:T(8,128)(2,1)} %qkv_own.3, bf16[576,1920]{1,0:T(8,128)(2,1)} %collective-permute-done.1.qkv_oth, bf16[6,8,16,1152]{3,2,1,0:T(8,128)(2,1)} %bitcast.23, bf16[512,1152]{1,0:T(8,128)(2,1)S(1)} %bitcast.19, ...), custom_call_target="tpu_custom_call" | custom-call | flops 4000000000 | bytes 10485760 | tf_op jit(solution)/shard_map/finish/pallas_call | solution.py:1156
  116.4 2.1 %all-to-all-done = bf16[16,16,896]{2,1,0:T(8,128)(2,1)S(1)} async-done(((bf16[16,16,896]{2,1,0:T(8,128)(2,1)}), bf16[16,16,896]{2,1,0:T(8,128)(2,1)S(1)}, u32[]{:S(2)}, u32[]{:S(2)}) %all-to-all-start) | async-done | bytes 458784 | tf_op jit(solution)/shard_map/all_to_all | solution.py:1358
  118.6 0.6 collect.1
  119.2 0.1 collective-permute-start.10
  119.2 1.5 %collective-permute-done.10.other = f32[4,16,896]{2,1,0:T(8,128)S(1)} collective-permute-done((f32[4,16,896]{2,1,0:T(8,128)S(1)}, f32[4,16,896]{2,1,0:T(8,128)S(1)}, u32[]{:S(2)}, u32[]{:S(2)}) %collective-permute-start.10) | collective-permute-done | bytes 229408 | tf_op jit(solution)/shard_map/ppermute | solution.py:1283
  120.7 1.0 deliver.1
  (7 shorter events, 0.0 us)
Async XLA Ops:
  0.6 1.8 %copy-start = (bf16[8,3072,16]{1,2,0:T(8,128)(2,1)S(1)}, bf16[8,3072,16]{1,2,0:T(8,128)(2,1)}, u32[]{:S(2)}) copy-start(bf16[8,3072,16]{1,2,0:T(8,128)(2,1)} %param.24) | copy-start | bytes 2359300
  0.7 7.4 %copy-start.9 = (bf16[2,576]{1,0:T(2,128)(2,1)S(1)}, bf16[2,576]{1,0:T(2,128)(2,1)}, u32[]{:S(2)}) copy-start(bf16[2,576]{1,0:T(2,128)(2,1)} %gains_own.5) | copy-start | bytes 6916
  0.7 7.1 %copy-start.2 = (bf16[576,1152]{1,0:T(8,128)(2,1)S(1)}, bf16[576,1152]{1,0:T(8,128)(2,1)}, u32[]{:S(2)}) copy-start(bf16[576,1152]{1,0:T(8,128)(2,1)} %wo_own.1) | copy-start | bytes 3981316
  0.7 7.4 %copy-start.6 = (bf16[3,8,16,1152]{3,2,1,0:T(8,128)(2,1)S(1)}, bf16[3,8,16,1152]{3,2,1,0:T(8,128)(2,1)}, u32[]{:S(2)}) copy-start(bf16[3,8,16,1152]{3,2,1,0:T(8,128)(2,1)} %upper_width.5) | copy-start | bytes 2654212
  0.7 7.4 %copy-start.7 = (bf16[2,8,16,384]{3,2,1,0:T(8,128)(2,1)S(1)}, bf16[2,8,16,384]{3,2,1,0:T(8,128)(2,1)}, u32[]{:S(2)}) copy-start(bf16[2,8,16,384]{3,2,1,0:T(8,128)(2,1)} %upper_keys.3) | copy-start | bytes 589828
  0.7 7.4 %copy-start.8 = (s32[1,1024]{1,0:T(1,128)S(1)}, s32[1,1024]{1,0:T(1,128)}, u32[]{:S(2)}) copy-start(s32[1,1024]{1,0:T(1,128)} %segments.1) | copy-start | bytes 12292
  0.7 6.5 %collective-permute-start.1 = (bf16[576,1920]{1,0:T(8,128)(2,1)}, bf16[576,1920]{1,0:T(8,128)(2,1)}, u32[]{:S(2)}, u32[]{:S(2)}) collective-permute-start(bf16[576,1920]{1,0:T(8,128)(2,1)} %qkv_own.3), channel_id=1, source_target_pairs={{0,16},{16,0},{1,17},{17,1},{2,18},{18,2},{3,19},{19,3},{4,20},{20... | collective-permute-start | bytes 6635528 | tf_op jit(solution)/shard_map/ppermute | solution.py:1283
  1.2 6.0 %collective-permute-start = (bf16[512,1152]{1,0:T(8,128)(2,1)}, bf16[512,1152]{1,0:T(8,128)(2,1)}, u32[]{:S(2)}, u32[]{:S(2)}) collective-permute-start(bf16[512,1152]{1,0:T(8,128)(2,1)} %bitcast.16), channel_id=1, source_target_pairs={{0,16},{16,0},{1,17},{17,1},{2,18},{18,2},{3,19},{19,3},{4,20},{20... | collective-permute-start | bytes 3538952 | tf_op jit(solution)/shard_map/ppermute | solution.py:1283
  1.3 4.1 %collective-permute-start.2 = (bf16[2,576]{1,0:T(2,128)(2,1)}, bf16[2,576]{1,0:T(2,128)(2,1)S(1)}, u32[]{:S(2)}, u32[]{:S(2)}) collective-permute-start(bf16[2,576]{1,0:T(2,128)(2,1)} %gains_own.5), channel_id=1, source_target_pairs={{0,16},{16,0},{1,17},{17,1},{2,18},{18,2},{3,19},{19,3},{4,20},{20... | collective-permute-start | bytes 6920 | tf_op jit(solution)/shard_map/ppermute | solution.py:1283
  7.2 24.3 %collective-permute-start.5 = (bf16[576,6144]{1,0:T(8,128)(2,1)}, bf16[576,6144]{1,0:T(8,128)(2,1)}, u32[]{:S(2)}, u32[]{:S(2)}) collective-permute-start(bf16[576,6144]{1,0:T(8,128)(2,1)} %wgu_own.1), channel_id=1, source_target_pairs={{0,16},{16,0},{1,17},{17,1},{2,18},{18,2},{3,19},{19,3},{4,20},{20... | collective-permute-start | bytes 21233672 | tf_op jit(solution)/shard_map/ppermute | solution.py:1283
  7.6 23.9 %collective-permute-start.6 = (bf16[1536,1152]{1,0:T(8,128)(2,1)}, bf16[1536,1152]{1,0:T(8,128)(2,1)}, u32[]{:S(2)}, u32[]{:S(2)}) collective-permute-start(bf16[1536,1152]{1,0:T(8,128)(2,1)} %wd_own.1), channel_id=1, source_target_pairs={{0,16},{16,0},{1,17},{17,1},{2,18},{18,2},{3,19},{19,3},{4,20},{20... | collective-permute-start | bytes 10616840 | tf_op jit(solution)/shard_map/ppermute | solution.py:1283
  7.7 23.8 %collective-permute-start.4 = (bf16[576,1152]{1,0:T(8,128)(2,1)S(1)}, bf16[576,1152]{1,0:T(8,128)(2,1)S(1)}, u32[]{:S(2)}, u32[]{:S(2)}) collective-permute-start(bf16[576,1152]{1,0:T(8,128)(2,1)S(1)} %copy-done.2), channel_id=1, source_target_pairs={{0,16},{16,0},{1,17},{17,1},{2,18},{18,2},{3,19},{19,3},{4,20},{20... | collective-permute-start | bytes 3981320 | tf_op jit(solution)/shard_map/ppermute | solution.py:1283
  8.1 23.4 %copy-start.3 = (bf16[1,512,1152]{2,1,0:T(8,128)(2,1)S(1)}, bf16[1,512,1152]{2,1,0:T(8,128)(2,1)}, u32[]{:S(2)}) copy-start(bf16[1,512,1152]{2,1,0:T(8,128)(2,1)} %param.15) | copy-start | bytes 3538948
  8.1 23.4 %copy-start.4 = (bf16[1,512,1152]{2,1,0:T(8,128)(2,1)S(1)}, bf16[1,512,1152]{2,1,0:T(8,128)(2,1)}, u32[]{:S(2)}) copy-start(bf16[1,512,1152]{2,1,0:T(8,128)(2,1)} %param.14) | copy-start | bytes 3538948
  29.3 2.2 %collective-permute-start.3 = (bf16[512,640]{1,0:T(8,128)(2,1)S(1)}, bf16[512,640]{1,0:T(8,128)(2,1)S(1)}, u32[]{:S(2)}, u32[]{:S(2)}) collective-permute-start(bf16[512,640]{1,0:T(8,128)(2,1)S(1)} %get-tuple-element.51), channel_id=1, source_target_pairs={{0,16},{16,0},{1,17},{17,1},{2,18},{18,2},{3,19},{19,3},{4,20},{20... | collective-permute-start | bytes 1966088 | tf_op jit(solution)/shard_map/ppermute | solution.py:1283
  71.5 2.5 %collective-permute-start.7 = (bf16[640,512]{1,0:T(8,128)(2,1)S(1)}, bf16[640,512]{1,0:T(8,128)(2,1)S(1)}, u32[]{:S(2)}, u32[]{:S(2)}) collective-permute-start(bf16[640,512]{1,0:T(8,128)(2,1)S(1)} %get-tuple-element.58), channel_id=1, source_target_pairs={{0,16},{16,0},{1,17},{17,1},{2,18},{18,2},{3,19},{19,3},{4,20},{20... | collective-permute-start | bytes 1966088 | tf_op jit(solution)/shard_map/ppermute | solution.py:1283
  71.7 2.3 %collective-permute-start.8 = (bf16[256,512]{1,0:T(8,128)(2,1)S(1)}, bf16[256,512]{1,0:T(8,128)(2,1)S(1)}, u32[]{:S(2)}, u32[]{:S(2)}) collective-permute-start(bf16[256,512]{1,0:T(8,128)(2,1)S(1)} %get-tuple-element.69), channel_id=1, source_target_pairs={{0,16},{16,0},{1,17},{17,1},{2,18},{18,2},{3,19},{19,3},{4,20},{20... | collective-permute-start | bytes 786440 | tf_op jit(solution)/shard_map/ppermute | solution.py:1283
  95.9 8.4 %collective-permute-start.9 = (bf16[512,1280]{1,0:T(8,128)(2,1)}, bf16[512,1280]{1,0:T(8,128)(2,1)S(1)}, u32[]{:S(2)}, u32[]{:S(2)}) collective-permute-start(bf16[512,1280]{1,0:T(8,128)(2,1)} %get-tuple-element.76), channel_id=1, source_target_pairs={{0,16},{16,0},{1,17},{17,1},{2,18},{18,2},{3,19},{19,3},{4,20},{20... | collective-permute-start | bytes 3932168 | tf_op jit(solution)/shard_map/ppermute | solution.py:1283
  96.1 22.4 %all-to-all-start = ((bf16[16,16,896]{2,1,0:T(8,128)(2,1)}), bf16[16,16,896]{2,1,0:T(8,128)(2,1)S(1)}, u32[]{:S(2)}, u32[]{:S(2)}) async-start(bf16[16,16,896]{2,1,0:T(8,128)(2,1)} %bitcast.6), calls=%async_computation | async-start | bytes 917504 | tf_op jit(solution)/shard_map/all_to_all | solution.py:1358
  104.4 1.3 %copy-start.5 = (bf16[1,512,1152]{2,1,0:T(8,128)(2,1)S(1)}, bf16[1,512,1152]{2,1,0:T(8,128)(2,1)}, u32[]{:S(2)}) copy-start(bf16[1,512,1152]{2,1,0:T(8,128)(2,1)} %param.14) | copy-start | bytes 3538948
  105.7 1.3 %copy-start.10 = (bf16[512,1280]{1,0:T(8,128)(2,1)S(1)}, bf16[512,1280]{1,0:T(8,128)(2,1)}, u32[]{:S(2)}) copy-start(bf16[512,1280]{1,0:T(8,128)(2,1)} %get-tuple-element.75.dy_in) | copy-start | bytes 3932164
  107.0 14.7 %copy-start.1 = (bf16[8,3072,16]{1,2,0:T(8,128)(2,1)S(1)}, bf16[8,3072,16]{1,2,0:T(8,128)(2,1)}, u32[]{:S(2)}) copy-start(bf16[8,3072,16]{1,2,0:T(8,128)(2,1)} %param.24) | copy-start | bytes 2359300
  119.2 1.6 %collective-permute-start.10 = (f32[4,16,896]{2,1,0:T(8,128)S(1)}, f32[4,16,896]{2,1,0:T(8,128)S(1)}, u32[]{:S(2)}, u32[]{:S(2)}) collective-permute-start(f32[4,16,896]{2,1,0:T(8,128)S(1)} %get-tuple-element.81), channel_id=1, source_target_pairs={{0,16},{16,0},{1,17},{17,1},{2,18},{18,2},{3,19},{19,3},{4,20},{20... | collective-permute-start | bytes 688136 | tf_op jit(solution)/shard_map/ppermute | solution.py:1283

commit v4 on v3

--- a/solution.py
+++ b/solution.py
@@ -649,11 +649,15 @@
     for load in second + third:
         load.wait()
     start(0, 0)
-    made = nn(o_own[...], wout[0]) + nn(o_oth[...], wout[1])
-    inner_out = made[:, D:].astype(bf16)
-    middle[...] = tok[...].astype(f32) + made[:, :D] + nn(inner_out, b_out[...])
-    scale = lax.rsqrt(jnp.mean(middle[...] * middle[...], axis=-1, keepdims=True) + epsilon)
-    normed[:, :D] = (middle[...] * scale * gain).astype(bf16)
+    count = tok.shape[0] // 2
+    spans = [slice(0, count), slice(count, 2 * count)]
+    mades = [nn(o_own[span, :], wout[0]) + nn(o_oth[span, :], wout[1]) for span in spans]
+    inner_out = jnp.concatenate([made[:, D:].astype(bf16) for made in mades], axis=0)
+    for span, made in zip(spans, mades):
+        rows_mid = tok[span, :].astype(f32) + made[:, :D] + nn(inner_out[span, :], b_out[...])
+        middle[span, :] = rows_mid
+        scale = lax.rsqrt(jnp.mean(rows_mid * rows_mid, axis=-1, keepdims=True) + epsilon)
+        normed[span, :D] = (rows_mid * scale * gain).astype(bf16)
     inner_gu = nt(normed[:, :D], at_gu[...])
     normed[:, D:] = inner_gu.astype(bf16)
     z_gu_t[...] = inner_gu.T[: 2 * R, :].astype(bf16)

time: 122 us -> 122 us (level)
  no operation moved by 1% of the time
where the time goes in v4:
time: 122 us; the launch traced here: 121 us
  Pallas kernels  93.6 us (77%)
  waiting for transfers between devices  11.8 us (10%)
  starting transfers between devices  11.2 us (9%)
  local copies, waits for them, and re-layouts  3.18 us (3%)
  between operations  1.49 us (1%)
    pallas_call x1, Pallas kernels, feed(): pl.pallas_call(functools.partial(feed_kernel, reps), out_shape=[shape((ro...  39.5 us
    pallas_call x1, Pallas kernels, attend_back(): pl.pallas_call(functools.partial(attend_back_kernel, reps), out_shape=[sh...  21.9 us
    pallas_call x1, Pallas kernels, attend(): pl.pallas_call(attend_kernel, out_shape=[shape((rows, QW), bf16), shape((...  21.2 us
    ppermute x11, waiting for transfers between devices, per_device(): swap = lambda value: lax.ppermute(value, 'grp', SWAP)  9.66 us
    pallas_call x1, Pallas kernels, finish(): pl.pallas_call(finish_kernel, out_shape=jax.ShapeDtypeStruct((rows, D), b...  9.44 us
    all_to_all x1, starting transfers between devices, per_device(): received = lax.all_to_all(exchange, 'rep', 0, 0, tiled=True)  8.23 us
    ppermute x11, starting transfers between devices, per_device(): swap = lambda value: lax.ppermute(value, 'grp', SWAP)  2.95 us
    unnamed x22, local copies, waits for them, and re-layouts  2.63 us
  transfers between devices with their start and end apart: 12, of which 6 were waited for; matrix products, arithmetic and copies ran while one was open for 0% of the time, Pallas kernels for 25%

profile of v4, /device:TPU:0, one launch (start us, length us, event | category | flops | bytes accessed | tf_op | source)
XLA Modules:
  0.0 121.2 jit_solution(9725593291692568715)
XLA Ops:
  0.6 0.0 copy-start
  0.7 0.0 copy-start.9
  0.7 0.0 copy-start.2
  0.7 0.0 copy-start.6
  0.7 0.0 copy-start.7
  0.7 0.0 copy-start.8
  0.7 0.5 collective-permute-start.1
  1.2 0.1 collective-permute-start
  1.3 0.4 collective-permute-start.2
  2.4 0.0 copy-done
  2.4 0.4 copy.21
  2.8 0.2 pad.4.a_down
  3.0 2.4 %collective-permute-done.2.gains_oth = bf16[2,576]{1,0:T(2,128)(2,1)S(1)} collective-permute-done((bf16[2,576]{1,0:T(2,128)(2,1)}, bf16[2,576]{1,0:T(2,128)(2,1)S(1)}, u32[]{:S(2)}, u32[]{:S(2)}) %collective-permute-start.2) | collective-permute-done | bytes 2336 | tf_op jit(solution)/shard_map/ppermute | solution.py:1287
  5.4 1.8 %collective-permute-done.tok_oth = bf16[512,1152]{1,0:T(8,128)(2,1)} collective-permute-done((bf16[512,1152]{1,0:T(8,128)(2,1)}, bf16[512,1152]{1,0:T(8,128)(2,1)}, u32[]{:S(2)}, u32[]{:S(2)}) %collective-permute-start) | collective-permute-done | bytes 1179680 | tf_op jit(solution)/shard_map/ppermute | solution.py:1287
  7.2 0.0 collective-permute-done.1.qkv_oth
  7.2 0.4 collective-permute-start.5
  7.6 0.1 collective-permute-start.6
  7.7 0.0 copy-done.2
  7.7 0.4 collective-permute-start.4
  8.1 0.0 copy-done.9
  8.1 0.0 copy-done.6
  8.1 0.0 copy-done.7
  8.1 0.0 copy-start.3
  8.1 0.0 copy-start.4
  8.1 21.2 %attend.1 = (bf16[512,640]{1,0:T(8,128)(2,1)S(1)}, bf16[512,640]{1,0:T(8,128)(2,1)S(1)}, bf16[640,1024]{1,0:T(8,128)(2,1)}, bf16[256,1024]{1,0:T(8,128)(2,1)S(1)...) custom-call(s32[1]{0:T(128)} %copy.22.adapter, ...), custom_call_target="tpu_custom_call" | custom-call | flops 16000000000 | bytes 16777216 | tf_op jit(solution)/shard_map/attend/pallas_call | solution.py:423
  29.3 0.2 collective-permute-start.3
  29.5 2.0 %collective-permute-done.3.o_oth_in = bf16[512,640]{1,0:T(8,128)(2,1)S(1)} collective-permute-done((bf16[512,640]{1,0:T(8,128)(2,1)S(1)}, bf16[512,640]{1,0:T(8,128)(2,1)S(1)}, u32[]{:S(2)}, u32[]{:S(2)}) %collective-permute-start.3) | collective-permute-done | bytes 655392 | tf_op jit(solution)/shard_map/ppermute | solution.py:1287
  31.5 0.0 collective-permute-done.4.wo_oth
  31.5 0.0 collective-permute-done.6.wd_oth
  31.5 0.0 collective-permute-done.5.wgu_oth
  31.5 39.5 %feed.1 = (bf16[512,1152]{1,0:T(8,128)(2,1)}, f32[512,1152]{1,0:T(8,128)}, bf16[640,512]{1,0:T(8,128)(2,1)S(1)}, bf16[640,512]{1,0:T(8,128)(2,1)S(1)}, bf16[256,...) custom-call(s32[1]{0:T(128)} %copy.22.adapter, bf16[512,640]{1,0:T(8,128)(2,1)S(1)} %get-tuple-element.50.o_own_in, ...), custom_call_target="tpu_custom_call" | custom-call | flops 30000001024 | bytes 37748736 | tf_op jit(solution)/shard_map/feed/pallas_call | solution.py:754
  71.0 0.2 collective-permute-start.7
  71.2 0.4 collective-permute-start.8
  71.6 2.0 %collective-permute-done.8.pack_oth_in = bf16[256,512]{1,0:T(8,128)(2,1)S(1)} collective-permute-done((bf16[256,512]{1,0:T(8,128)(2,1)S(1)}, bf16[256,512]{1,0:T(8,128)(2,1)S(1)}, u32[]{:S(2)}, u32[]{:S(2)}) %collective-permute-start.8) | collective-permute-done | bytes 262176 | tf_op jit(solution)/shard_map/ppermute | solution.py:1287
  73.6 0.0 collective-permute-done.7.do_oth
  73.6 21.9 %attend_back.1 = (bf16[512,1280]{1,0:T(8,128)(2,1)}, bf16[512,1280]{1,0:T(8,128)(2,1)}, bf16[256,896]{1,0:T(8,128)(2,1)}) custom-call(s32[1]{0:T(128)} %copy.22.adapter, bf16[640,512]{1,0:T(8,128)(2,1)S(1)} %get-tuple-element.57.do_own, bf16[640,512]{1,0:T(8,128)(2,1)S(1)} %collective-permute-done.7.do_oth, bf16[704,1024]{1,0:T(8,128)(2,1)} %get-tuple-element.59.o_in, ...), custom_call_target="tpu_custom_call" | custom-call | flops 24000000000 | bytes 20971520 | tf_op jit(solution)/shard_map/attend_back/pallas_call | solution.py:1044
  95.5 0.2 collective-permute-start.9
  95.6 8.2 %all-to-all-start = ((bf16[16,16,896]{2,1,0:T(8,128)(2,1)}), bf16[16,16,896]{2,1,0:T(8,128)(2,1)S(1)}, u32[]{:S(2)}, u32[]{:S(2)}) async-start(bf16[16,16,896]{2,1,0:T(8,128)(2,1)} %bitcast.6), calls=%async_computation | async-start | bytes 917504 | tf_op jit(solution)/shard_map/all_to_all | solution.py:1362
  103.9 0.0 collective-permute-done.9.part_in
  103.9 0.0 copy-start.5
  103.9 1.3 %copy-done.5 = bf16[1,512,1152]{2,1,0:T(8,128)(2,1)S(1)} copy-done((bf16[1,512,1152]{2,1,0:T(8,128)(2,1)S(1)}, bf16[1,512,1152]{2,1,0:T(8,128)(2,1)}, u32[]{:S(2)}) %copy-start.5) | copy-done | bytes 1179672
  105.2 1.3 %copy-done.10 = bf16[512,1280]{1,0:T(8,128)(2,1)S(1)} copy-done((bf16[512,1280]{1,0:T(8,128)(2,1)S(1)}, bf16[512,1280]{1,0:T(8,128)(2,1)}, u32[]{:S(2)}) %copy-start.10) | copy-done | bytes 1310744
  106.5 9.4 %finish.1 = bf16[512,1152]{1,0:T(8,128)(2,1)} custom-call(s32[1]{0:T(128)} %copy.22.adapter, bf16[512,1280]{1,0:T(8,128)(2,1)S(1)} %copy-done.10, bf16[576,1920]{1,0:T(8,128)(2,1)} %qkv_own.3, bf16[576,1920]{1,0:T(8,128)(2,1)} %collective-permute-done.1.qkv_oth, bf16[6,8,16,1152]{3,2,1,0:T(8,128)(2,1)} %bitcast.23, bf16[512,1152]{1,0:T(8,128)(2,1)S(1)} %bitcast.19, ...), custom_call_target="tpu_custom_call" | custom-call | flops 4000000000 | bytes 10485760 | tf_op jit(solution)/shard_map/finish/pallas_call | solution.py:1160
  115.9 2.1 %all-to-all-done = bf16[16,16,896]{2,1,0:T(8,128)(2,1)S(1)} async-done(((bf16[16,16,896]{2,1,0:T(8,128)(2,1)}), bf16[16,16,896]{2,1,0:T(8,128)(2,1)S(1)}, u32[]{:S(2)}, u32[]{:S(2)}) %all-to-all-start) | async-done | bytes 458784 | tf_op jit(solution)/shard_map/all_to_all | solution.py:1362
  118.1 0.6 collect.1
  118.7 0.1 collective-permute-start.10
  118.8 1.5 %collective-permute-done.10.other = f32[4,16,896]{2,1,0:T(8,128)S(1)} collective-permute-done((f32[4,16,896]{2,1,0:T(8,128)S(1)}, f32[4,16,896]{2,1,0:T(8,128)S(1)}, u32[]{:S(2)}, u32[]{:S(2)}) %collective-permute-start.10) | collective-permute-done | bytes 229408 | tf_op jit(solution)/shard_map/ppermute | solution.py:1287
  120.2 1.0 deliver.1
  (7 shorter events, 0.0 us)
Async XLA Ops:
  0.6 1.8 %copy-start = (bf16[8,3072,16]{1,2,0:T(8,128)(2,1)S(1)}, bf16[8,3072,16]{1,2,0:T(8,128)(2,1)}, u32[]{:S(2)}) copy-start(bf16[8,3072,16]{1,2,0:T(8,128)(2,1)} %param.24) | copy-start | bytes 2359300
  0.7 7.4 %copy-start.9 = (bf16[2,576]{1,0:T(2,128)(2,1)S(1)}, bf16[2,576]{1,0:T(2,128)(2,1)}, u32[]{:S(2)}) copy-start(bf16[2,576]{1,0:T(2,128)(2,1)} %gains_own.5) | copy-start | bytes 6916
  0.7 7.1 %copy-start.2 = (bf16[576,1152]{1,0:T(8,128)(2,1)S(1)}, bf16[576,1152]{1,0:T(8,128)(2,1)}, u32[]{:S(2)}) copy-start(bf16[576,1152]{1,0:T(8,128)(2,1)} %wo_own.1) | copy-start | bytes 3981316
  0.7 7.4 %copy-start.6 = (bf16[3,8,16,1152]{3,2,1,0:T(8,128)(2,1)S(1)}, bf16[3,8,16,1152]{3,2,1,0:T(8,128)(2,1)}, u32[]{:S(2)}) copy-start(bf16[3,8,16,1152]{3,2,1,0:T(8,128)(2,1)} %upper_width.5) | copy-start | bytes 2654212
  0.7 7.4 %copy-start.7 = (bf16[2,8,16,384]{3,2,1,0:T(8,128)(2,1)S(1)}, bf16[2,8,16,384]{3,2,1,0:T(8,128)(2,1)}, u32[]{:S(2)}) copy-start(bf16[2,8,16,384]{3,2,1,0:T(8,128)(2,1)} %upper_keys.3) | copy-start | bytes 589828
  0.7 7.4 %copy-start.8 = (s32[1,1024]{1,0:T(1,128)S(1)}, s32[1,1024]{1,0:T(1,128)}, u32[]{:S(2)}) copy-start(s32[1,1024]{1,0:T(1,128)} %segments.1) | copy-start | bytes 12292
  0.7 6.5 %collective-permute-start.1 = (bf16[576,1920]{1,0:T(8,128)(2,1)}, bf16[576,1920]{1,0:T(8,128)(2,1)}, u32[]{:S(2)}, u32[]{:S(2)}) collective-permute-start(bf16[576,1920]{1,0:T(8,128)(2,1)} %qkv_own.3), channel_id=1, source_target_pairs={{0,16},{16,0},{1,17},{17,1},{2,18},{18,2},{3,19},{19,3},{4,20},{20... | collective-permute-start | bytes 6635528 | tf_op jit(solution)/shard_map/ppermute | solution.py:1287
  1.2 6.0 %collective-permute-start = (bf16[512,1152]{1,0:T(8,128)(2,1)}, bf16[512,1152]{1,0:T(8,128)(2,1)}, u32[]{:S(2)}, u32[]{:S(2)}) collective-permute-start(bf16[512,1152]{1,0:T(8,128)(2,1)} %bitcast.16), channel_id=1, source_target_pairs={{0,16},{16,0},{1,17},{17,1},{2,18},{18,2},{3,19},{19,3},{4,20},{20... | collective-permute-start | bytes 3538952 | tf_op jit(solution)/shard_map/ppermute | solution.py:1287
  1.3 4.1 %collective-permute-start.2 = (bf16[2,576]{1,0:T(2,128)(2,1)}, bf16[2,576]{1,0:T(2,128)(2,1)S(1)}, u32[]{:S(2)}, u32[]{:S(2)}) collective-permute-start(bf16[2,576]{1,0:T(2,128)(2,1)} %gains_own.5), channel_id=1, source_target_pairs={{0,16},{16,0},{1,17},{17,1},{2,18},{18,2},{3,19},{19,3},{4,20},{20... | collective-permute-start | bytes 6920 | tf_op jit(solution)/shard_map/ppermute | solution.py:1287
  7.2 24.3 %collective-permute-start.5 = (bf16[576,6144]{1,0:T(8,128)(2,1)}, bf16[576,6144]{1,0:T(8,128)(2,1)}, u32[]{:S(2)}, u32[]{:S(2)}) collective-permute-start(bf16[576,6144]{1,0:T(8,128)(2,1)} %wgu_own.1), channel_id=1, source_target_pairs={{0,16},{16,0},{1,17},{17,1},{2,18},{18,2},{3,19},{19,3},{4,20},{20... | collective-permute-start | bytes 21233672 | tf_op jit(solution)/shard_map/ppermute | solution.py:1287
  7.6 23.9 %collective-permute-start.6 = (bf16[1536,1152]{1,0:T(8,128)(2,1)}, bf16[1536,1152]{1,0:T(8,128)(2,1)}, u32[]{:S(2)}, u32[]{:S(2)}) collective-permute-start(bf16[1536,1152]{1,0:T(8,128)(2,1)} %wd_own.1), channel_id=1, source_target_pairs={{0,16},{16,0},{1,17},{17,1},{2,18},{18,2},{3,19},{19,3},{4,20},{20... | collective-permute-start | bytes 10616840 | tf_op jit(solution)/shard_map/ppermute | solution.py:1287
  7.7 23.8 %collective-permute-start.4 = (bf16[576,1152]{1,0:T(8,128)(2,1)S(1)}, bf16[576,1152]{1,0:T(8,128)(2,1)S(1)}, u32[]{:S(2)}, u32[]{:S(2)}) collective-permute-start(bf16[576,1152]{1,0:T(8,128)(2,1)S(1)} %copy-done.2), channel_id=1, source_target_pairs={{0,16},{16,0},{1,17},{17,1},{2,18},{18,2},{3,19},{19,3},{4,20},{20... | collective-permute-start | bytes 3981320 | tf_op jit(solution)/shard_map/ppermute | solution.py:1287
  8.1 23.4 %copy-start.3 = (bf16[1,512,1152]{2,1,0:T(8,128)(2,1)S(1)}, bf16[1,512,1152]{2,1,0:T(8,128)(2,1)}, u32[]{:S(2)}) copy-start(bf16[1,512,1152]{2,1,0:T(8,128)(2,1)} %param.15) | copy-start | bytes 3538948
  8.1 23.4 %copy-start.4 = (bf16[1,512,1152]{2,1,0:T(8,128)(2,1)S(1)}, bf16[1,512,1152]{2,1,0:T(8,128)(2,1)}, u32[]{:S(2)}) copy-start(bf16[1,512,1152]{2,1,0:T(8,128)(2,1)} %param.14) | copy-start | bytes 3538948
  29.3 2.2 %collective-permute-start.3 = (bf16[512,640]{1,0:T(8,128)(2,1)S(1)}, bf16[512,640]{1,0:T(8,128)(2,1)S(1)}, u32[]{:S(2)}, u32[]{:S(2)}) collective-permute-start(bf16[512,640]{1,0:T(8,128)(2,1)S(1)} %get-tuple-element.51), channel_id=1, source_target_pairs={{0,16},{16,0},{1,17},{17,1},{2,18},{18,2},{3,19},{19,3},{4,20},{20... | collective-permute-start | bytes 1966088 | tf_op jit(solution)/shard_map/ppermute | solution.py:1287
  71.0 2.5 %collective-permute-start.7 = (bf16[640,512]{1,0:T(8,128)(2,1)S(1)}, bf16[640,512]{1,0:T(8,128)(2,1)S(1)}, u32[]{:S(2)}, u32[]{:S(2)}) collective-permute-start(bf16[640,512]{1,0:T(8,128)(2,1)S(1)} %get-tuple-element.58), channel_id=1, source_target_pairs={{0,16},{16,0},{1,17},{17,1},{2,18},{18,2},{3,19},{19,3},{4,20},{20... | collective-permute-start | bytes 1966088 | tf_op jit(solution)/shard_map/ppermute | solution.py:1287
  71.2 2.3 %collective-permute-start.8 = (bf16[256,512]{1,0:T(8,128)(2,1)S(1)}, bf16[256,512]{1,0:T(8,128)(2,1)S(1)}, u32[]{:S(2)}, u32[]{:S(2)}) collective-permute-start(bf16[256,512]{1,0:T(8,128)(2,1)S(1)} %get-tuple-element.69), channel_id=1, source_target_pairs={{0,16},{16,0},{1,17},{17,1},{2,18},{18,2},{3,19},{19,3},{4,20},{20... | collective-permute-start | bytes 786440 | tf_op jit(solution)/shard_map/ppermute | solution.py:1287
  95.5 8.4 %collective-permute-start.9 = (bf16[512,1280]{1,0:T(8,128)(2,1)}, bf16[512,1280]{1,0:T(8,128)(2,1)S(1)}, u32[]{:S(2)}, u32[]{:S(2)}) collective-permute-start(bf16[512,1280]{1,0:T(8,128)(2,1)} %get-tuple-element.76), channel_id=1, source_target_pairs={{0,16},{16,0},{1,17},{17,1},{2,18},{18,2},{3,19},{19,3},{4,20},{20... | collective-permute-start | bytes 3932168 | tf_op jit(solution)/shard_map/ppermute | solution.py:1287
  95.6 22.4 %all-to-all-start = ((bf16[16,16,896]{2,1,0:T(8,128)(2,1)}), bf16[16,16,896]{2,1,0:T(8,128)(2,1)S(1)}, u32[]{:S(2)}, u32[]{:S(2)}) async-start(bf16[16,16,896]{2,1,0:T(8,128)(2,1)} %bitcast.6), calls=%async_computation | async-start | bytes 917504 | tf_op jit(solution)/shard_map/all_to_all | solution.py:1362
  103.9 1.3 %copy-start.5 = (bf16[1,512,1152]{2,1,0:T(8,128)(2,1)S(1)}, bf16[1,512,1152]{2,1,0:T(8,128)(2,1)}, u32[]{:S(2)}) copy-start(bf16[1,512,1152]{2,1,0:T(8,128)(2,1)} %param.14) | copy-start | bytes 3538948
  105.2 1.3 %copy-start.10 = (bf16[512,1280]{1,0:T(8,128)(2,1)S(1)}, bf16[512,1280]{1,0:T(8,128)(2,1)}, u32[]{:S(2)}) copy-start(bf16[512,1280]{1,0:T(8,128)(2,1)} %get-tuple-element.75.dy_in) | copy-start | bytes 3932164
  106.5 14.7 %copy-start.1 = (bf16[8,3072,16]{1,2,0:T(8,128)(2,1)S(1)}, bf16[8,3072,16]{1,2,0:T(8,128)(2,1)}, u32[]{:S(2)}) copy-start(bf16[8,3072,16]{1,2,0:T(8,128)(2,1)} %param.24) | copy-start | bytes 2359300
  118.7 1.6 %collective-permute-start.10 = (f32[4,16,896]{2,1,0:T(8,128)S(1)}, f32[4,16,896]{2,1,0:T(8,128)S(1)}, u32[]{:S(2)}, u32[]{:S(2)}) collective-permute-start(f32[4,16,896]{2,1,0:T(8,128)S(1)} %get-tuple-element.81), channel_id=1, source_target_pairs={{0,16},{16,0},{1,17},{17,1},{2,18},{18,2},{3,19},{19,3},{4,20},{20... | collective-permute-start | bytes 688136 | tf_op jit(solution)/shard_map/ppermute | solution.py:1287
